TPU v7x, 512 devices: a whole 4x4x16 slice. The times are simulated.
512 devices in a mesh: scen: 64 (over x_hi, z, core), node: 8 (over x_lo, y).
Axes of the slice: x: 4 (x_hi: 2, x_lo: 2; x = x_hi * 2 + x_lo), y: 4, z: 16, core: 2. Of those that a mesh axis runs over, the one named last changes fastest.
Arguments:
- link_blocks: float32 [2048, 256, 512], P(('scen', 'node'))
- inverse_blocks: float32 [2048, 256, 256], P(('scen', 'node')), as said below
- block_rows: int32 [2048], P(('scen', 'node')), may hold values from 64 to 256, as said below
- node_of: int32 [2048], P(('scen', 'node')), may hold values from 0 to 15, as said below
- slot_count: int32 [512], P(('scen', 'node')), may hold values from 1 to 4, as said below
- node_diag: float32 [16, 512], P('node'), may hold values from 0.5 to 2
- first_link: float32 [16, 512, 512], P('node', None, 'scen'), may hold values from -0.09375 to 0.09375
- first_diag: float32 [512], P('scen'), may hold values from 0.5 to 2
Outputs:
- node_factor: float32 [16, 512, 512], P('node', 'scen')
- first_schur: float32 [512, 512], P('scen')
Inputs may be any that keep to these rules, and one draw needn't show every extreme that they name: `inverse_blocks`: each block is symmetric and positive definite. `block_rows`: rows at or past this count are padding. `node_of`: every slot held by a device names a node of that device's group: with g the device's index along node, nodes g * 2 to g * 2 + 1. `slot_count`: slots of a device at or past its count are ignored.
All inputs are finite; a program needn't handle non-finite values.
Results may differ from a plain program's by a relative error of at most 0.0003.
Values sent between devices are 32-bit elements; how exact they have to be, the bound alone decides.
A program may use at most 64 MiB of HBM per device.

v0:
```python
import jax
import jax.numpy as jnp
from jax import lax
from jax.sharding import PartitionSpec as P


def slot_term(link_block, inverse_block, live_rows):
    row_ids = lax.broadcasted_iota(jnp.int32, (link_block.shape[0], 1), 0)
    masked = jnp.where(row_ids < live_rows, link_block, jnp.zeros_like(link_block))
    scaled = jnp.dot(
        inverse_block, masked, precision=lax.Precision.HIGHEST, preferred_element_type=jnp.float32
    )
    return lax.dot_general(
        masked,
        scaled,
        (((0,), (0,)), ((), ())),
        precision=lax.Precision.HIGHEST,
        preferred_element_type=jnp.float32,
    )


def shards(
    link_blocks, inverse_blocks, block_rows, node_of, slot_count, node_diag, first_link, first_diag
):
    node_groups = node_diag.shape[0]
    link_width = link_blocks.shape[2]
    scen_devices = lax.axis_size("scen")
    row_share = link_width // scen_devices
    col_share = first_link.shape[2]
    first_width = col_share * scen_devices
    scen_place = lax.axis_index("scen")
    node_start = lax.axis_index("node") * node_groups

    def add_slot(slot_index, partial_value):
        contrib = slot_term(
            link_blocks[slot_index], inverse_blocks[slot_index], block_rows[slot_index]
        )
        local_node = node_of[slot_index] - node_start
        current = lax.dynamic_index_in_dim(partial_value, local_node, 0, keepdims=False)
        return lax.dynamic_update_index_in_dim(partial_value, current + contrib, local_node, 0)

    partial_value = lax.fori_loop(
        0, slot_count[0], add_slot, jnp.zeros((node_groups, link_width, link_width), jnp.float32)
    )
    identity = jnp.eye(link_width, dtype=jnp.float32)
    row_terms = lax.psum_scatter(partial_value, "scen", scatter_dimension=1, tiled=True)
    gathered = lax.all_gather(row_terms, "scen", axis=1, tiled=True)
    factor = jnp.linalg.cholesky(gathered + node_diag[:, :, None] * identity)
    node_factor = lax.dynamic_slice_in_dim(factor, scen_place * row_share, row_share, 1)
    solved_own = lax.linalg.triangular_solve(factor, first_link, left_side=True, lower=True)
    row_block = jnp.einsum(
        "gwa,gwb->ab",
        solved_own,
        lax.all_gather(solved_own, "scen", axis=2, tiled=True),
        precision=lax.Precision.HIGHEST,
    )
    summed = lax.psum(row_block, "node")
    diag_rows = (
        lax.broadcasted_iota(jnp.int32, (col_share, first_width), 0) + scen_place * col_share
    )
    diag_cols = lax.broadcasted_iota(jnp.int32, (col_share, first_width), 1)
    first_schur = summed + jnp.where(diag_rows == diag_cols, first_diag[:, None], 0.0)
    return (node_factor, first_schur)


def solution(mesh):
    in_specs = (
        P(("scen", "node"), None, None),
        P(("scen", "node"), None, None),
        P(("scen", "node")),
        P(("scen", "node")),
        P(("scen", "node")),
        P("node", None),
        P("node", None, "scen"),
        P("scen"),
    )
    out_specs = (P("node", "scen", None), P("scen", None))
    return jax.shard_map(shards, mesh=mesh, in_specs=in_specs, out_specs=out_specs, check_vma=False)
```

profile of v0, /device:TPU:1, one launch (start us, length us, event | category | flops | bytes accessed | tf_op | source)
XLA Modules:
  0.0 1202.3 jit_solution(10772225185610107802)
XLA Ops:
  7.2 0.5 broadcast_in_dim.41.clone
  7.8 18.3 %while.11 = (s32[]{:T(128)}, f32[2,512,512]{2,0,1:T(2,128)S(1)}, s32[]{:T(128)}, s32[4]{0:T(128)S(1)}, s32[]{:T(128)}, /*index=5*/s32[4]{0:T(128)S(1)}, f32[4,25...) while((s32[]{:T(128)}, f32[2,512,512]{2,0,1:T(2,128)S(1)}, ...), condition=%wide.region_1.2_spmd, body=%wide.region_0.1_spmd.sunk | while | flops 1208484096 | bytes 19139080 | solution.py:42
  8.5 0.7 dynamic_slice.45
  9.9 0.9 constant_dynamic-slice_fusion.6
  10.8 0.7 dynamic_slice.44
  11.5 0.7 iota_compare_fusion.7
  12.2 1.7 fusion.64
  13.9 1.1 fusion.65
  15.0 1.1 copy.74
  16.1 9.4 dynamic_update_slice.5
  26.1 1.3 copy-done
  27.5 1.3 dynamic-slice.4
  29.4 581.0 %all-reduce.4.cloned.1.call-done = f32[2,512,512]{2,0,1:T(2,128)} async-done(((f32[2,512,512]{2,0,1:T(2,128)}), f32[2,512,512]{2,0,1:T(2,128)}) %all-reduce.4.cloned.1.call-update) | async-done | bytes 2097168
  610.4 1.4 constant_dynamic-slice_fusion.3
  611.8 0.3 all-gather.5.cloned.1.call-start
  612.2 0.1 iota_compare_fusion.2
  612.3 0.1 fusion.17
  612.5 140.0 %all-gather.3.cloned.1.call-done = f32[2,512,512]{2,0,1:T(2,128)} async-done(((f32[2,8,512]{2,0,1:T(2,128)}), f32[2,512,512]{2,0,1:T(2,128)}) %all-gather.3.cloned.1.call-update) | async-done | bytes 2097168 | tf_op jit(solution)/shard_map/all_gather | solution.py:47
  752.5 2.7 copy.38
  755.2 1.7 multiply_add_fusion
  757.0 2.9 copy.39
  759.9 2.2 fusion.16
  762.1 1.3 copy-done.2
  763.5 23.5 %custom-call.34 = f32[2,128,128]{2,1,0:T(8,128)S(1)} custom-call(f32[2,128,128]{2,1,0:T(8,128)S(1)} %cholesky.271), custom_call_target="Cholesky" | custom-call | tf_op jit(solution)/shard_map/jit(cholesky)/cholesky | solution.py:48
  786.9 0.3 cholesky.232
  787.2 19.7 %custom-call.35 = f32[2,1,128,128]{2,3,1,0:T(8,128)S(1)} custom-call(f32[2,1,128,128]{3,2,1,0:T(8,128)S(1)} %select_bitcast_fusion.2), custom_call_target="InvertDiagBlocksLowerTriangular" | custom-call | tf_op jit(solution)/shard_map/jit(cholesky)/cholesky | solution.py:48
  806.9 1.5 constant_dynamic-update-slice_fusion.3
  808.4 1.5 convolution_subtract_fusion
  809.9 24.0 %custom-call.36 = f32[2,128,128]{2,1,0:T(8,128)S(1)} custom-call(f32[2,128,128]{2,1,0:T(8,128)S(1)} %cholesky.275), custom_call_target="Cholesky" | custom-call | tf_op jit(solution)/shard_map/jit(cholesky)/cholesky | solution.py:48
  833.9 19.7 %custom-call.37 = f32[2,1,128,128]{2,3,1,0:T(8,128)S(1)} custom-call(f32[2,1,128,128]{3,2,1,0:T(8,128)S(1)} %get-tuple-element.89), custom_call_target="InvertDiagBlocksLowerTriangular" | custom-call | tf_op jit(solution)/shard_map/jit(cholesky)/cholesky | solution.py:48
  853.6 0.4 convolution_dynamic-update-slice_fusion
  854.0 1.6 convolution_subtract_fusion.1
  855.6 23.5 %custom-call.38 = f32[2,128,128]{2,1,0:T(8,128)S(1)} custom-call(f32[2,128,128]{2,1,0:T(8,128)S(1)} %cholesky.280), custom_call_target="Cholesky" | custom-call | tf_op jit(solution)/shard_map/jit(cholesky)/cholesky | solution.py:48
  879.1 19.8 %custom-call.39 = f32[2,1,128,128]{2,3,1,0:T(8,128)S(1)} custom-call(f32[2,1,128,128]{3,2,1,0:T(8,128)S(1)} %get-tuple-element.87), custom_call_target="InvertDiagBlocksLowerTriangular" | custom-call | tf_op jit(solution)/shard_map/jit(cholesky)/cholesky | solution.py:48
  898.9 0.3 convolution_dynamic-update-slice_fusion.1
  899.2 1.5 convolution_subtract_fusion.2
  900.7 23.5 %custom-call.40 = f32[2,128,128]{2,1,0:T(8,128)S(1)} custom-call(f32[2,128,128]{2,1,0:T(8,128)S(1)} %convolution_subtract_fusion.2), custom_call_target="Cholesky" | custom-call | tf_op jit(solution)/shard_map/jit(cholesky)/cholesky | solution.py:48
  924.3 0.1 compare_reduce_fusion.2
  924.4 0.2 compare_reduce_fusion
  924.6 2.6 broadcast_select_fusion
  927.2 14.0 %while.12 = (s32[]{:T(128)}, f32[2,512,512]{2,1,0:T(8,128)}, s32[4,2]{0,1:T(2,128)S(1)}, f32[4,2,128,128]{3,2,0,1:T(8,128)}, s32[]{:T(128)}) while((s32[]{:T(128)}, f32[2,512,512]{2,1,0:T(8,128)}, s32[4,2]{0,1:T(2,128)S(1)}, f32[4,2,128,128]{3,2,0,1:T(8,128)}, s32[]{:T(128)}) %tuple.49), condition=%wide.while_cond, body=%wide.while_body.sunk | while | flops 2 | bytes 263777 | solution.py:50
  927.2 0.1 constant_dynamic-slice_fusion.7
  927.3 0.5 fusion.66
  927.8 2.9 bitcast_dynamic-update-slice_fusion.2
  930.8 0.5 fusion.66
  931.4 2.9 bitcast_dynamic-update-slice_fusion.2
  934.3 0.5 fusion.66
  934.9 2.9 bitcast_dynamic-update-slice_fusion.2
  937.9 0.5 fusion.66
  938.4 2.9 bitcast_dynamic-update-slice_fusion.2
  941.2 79.6 %custom-call.41 = f32[2,4,128,128]{2,3,1,0:T(8,128)S(1)} custom-call(f32[2,4,128,128]{3,2,1,0:T(8,128)} %bitcast.96), custom_call_target="InvertDiagBlocksLowerTriangular" | custom-call | tf_op jit(solution)/shard_map/triangular_solve | solution.py:50
  1020.9 0.2 fusion.30
  1021.1 1.2 convolution_subtract_fusion.4
  1022.4 0.2 fusion.29
  1022.6 1.3 convolution_subtract_fusion.3
  1023.9 0.2 fusion.27
  1024.1 1.5 convolution_subtract_fusion.5
  1025.7 0.2 fusion.26
  1025.9 0.6 pad_maximum_fusion
  1026.6 1.4 constant_dynamic-slice_fusion.2
  1027.9 137.2 %all-gather.5.cloned.1.call-done = f32[2,512,512]{1,2,0:T(8,128)} async-done(((f32[2,512,8]{1,2,0:T(8,128)}), f32[2,512,512]{1,2,0:T(8,128)}) %all-gather.5.cloned.1.call-update) | async-done | bytes 2097168 | tf_op jit(solution)/shard_map/all_gather | solution.py:54
  1165.2 3.4 convolution_bitcast_fusion
  1168.6 26.3 %psum.7 = f32[8,512]{1,0:T(8,128)S(1)} all-reduce(f32[8,512]{1,0:T(8,128)S(1)} %convolution_bitcast_fusion), channel_id=1, replica_groups=mesh['scen'=64,'node'=8] {'node'}, use_global_device_ids=true, to_apply=%region_11.12 | all-reduce | flops 4096 | bytes 32768 | tf_op jit(solution)/shard_map/psum | solution.py:57
  1194.8 0.7 select_add_fusion
  (36 shorter events, 0.6 us)
Async XLA Ops:
  7.2 0.7 copy-start.7
  7.2 0.7 copy-start.6
  7.2 603.3 %all-reduce.4.cloned.1.call-start = ((), (), s32[]{:S(2)}) async-start(), calls=%async_computation.2 | async-start | bytes 4194304
  9.9 2.3 copy-start.1
  26.1 1.3 copy-start
  27.4 725.1 %all-gather.3.cloned.1.call-start = ((), (), s32[]{:S(2)}) async-start(), calls=%async_computation | async-start | bytes 2129920 | tf_op jit(solution)/shard_map/all_gather | solution.py:47
  611.8 553.3 %all-gather.5.cloned.1.call-start = ((), (), s32[]{:S(2)}) async-start(), calls=%async_computation.1 | async-start | bytes 2129920 | tf_op jit(solution)/shard_map/all_gather | solution.py:54
  612.5 142.8 %copy-start.4 = (f32[2,512]{1,0:T(2,128)S(1)}, f32[2,512]{1,0:T(2,128)}, u32[]{:S(2)}) copy-start(f32[2,512]{1,0:T(2,128)} %param.15) | copy-start | bytes 12292
  762.1 1.4 copy-start.2
  924.6 96.3 %copy-start.3 = (f32[2,512,8]{1,2,0:T(8,128)S(1)}, f32[2,512,8]{1,2,0:T(8,128)}, u32[]{:S(2)}) copy-start(f32[2,512,8]{1,2,0:T(8,128)} %param.16) | copy-start | bytes 98308
  941.2 253.6 %copy-start.5 = (f32[8]{0:T(128)S(1)}, f32[8]{0:T(128)}, u32[]{:S(2)}) copy-start(f32[8]{0:T(128)} %param.17) | copy-start | bytes 100
Sparse Core Ops, SparseCore 0:
  27.5 582.8 all-reduce.3
  614.8 137.6 all-gather.2
  1026.7 138.4 all-gather.4
where the time goes:
time: 1210 us; the launch traced here: 1200 us
  waiting for transfers between devices  858 us (71%)
  other arithmetic  242 us (20%)
  local copies, waits for them, and re-layouts  39.9 us (3%)
  blocking collectives  26.3 us (2%)
  matrix products  17.9 us (1%)
  between operations  14.9 us (1%)
    unnamed x4, waiting for transfers between devices  581 us
    another operation x16, other arithmetic, shards(): factor = jnp.linalg.cholesky(gathered + node_diag[:, :, None] * identity)  154 us
    all_gather x1, waiting for transfers between devices, shards(): gathered = lax.all_gather(row_terms, 'scen', axis=1, tiled=True)  140 us
    all_gather x1, waiting for transfers between devices, shards(): lax.all_gather(solved_own, 'scen', axis=2, tiled=True)  137 us
    another operation x4, other arithmetic, shards(): lax.linalg.triangular_solve(factor, first_link, left_side=True, lower=True)  82.9 us
    psum x1, blocking collectives, shards(): summed = lax.psum(row_block, 'node')  26.3 us
  transfers between devices with their start and end apart: 3, of which 3 were waited for; matrix products, arithmetic and copies ran while one was open for 0% of the time, Pallas kernels for 0%

commit v1 on v0

v1 whole, which is shorter than its diff:
```python
import functools

import jax
import jax.numpy as jnp
from jax import lax
from jax.experimental import pallas as pl
from jax.experimental.pallas import tpu as pltpu
from jax.sharding import PartitionSpec as P

f32, bf16 = jnp.float32, jnp.bfloat16
NN = (((1,), (0,)), ((), ()))
NT = (((1,), (1,)), ((), ()))
TN = (((0,), (0,)), ((), ()))
Z = 16
K = 4
OFF = (0, 4, 7, 9)
TILES = 10
MESH = pl.DeviceIdType.MESH


def split(x):
    high = x.astype(bf16)
    return high, (x - high.astype(f32)).astype(bf16)


def mm(a, b, dims):
    def one(p, q):
        return lax.dot_general(p, q, dims, preferred_element_type=f32)

    return one(a[0], b[0]) + (one(a[0], b[1]) + one(a[1], b[0]))


def sub_row(x, k):
    return jnp.broadcast_to(x[k : k + 1, :], (8, 128))


def lane_col(x, j):
    return jnp.broadcast_to(x[:, j : j + 1], (8, 128))


def tree(terms):
    terms = list(terms)
    while len(terms) > 1:
        terms = [
            terms[i] + terms[i + 1] if i + 1 < len(terms) else terms[i]
            for i in range(0, len(terms), 2)
        ]
    return terms[0]


def eliminate(cols, sub):
    w = [jnp.zeros((8, 128), f32)] * 8
    n = list(cols)
    for i in range(8):
        hit = sub == i
        row = [sub_row(n[k], i) for k in range(8)]
        p = 1.0 / row[i]
        r = lax.rsqrt(row[i])
        m = jnp.where(hit, 0.0, n[i])
        for k in range(8):
            if k == i:
                continue
            c = row[k] * p
            if k < i:
                w[k] = jnp.where(hit, row[k] * r, w[k])
            n[k] = jnp.where(hit, c, n[k] - m * c)
        w[i] = jnp.where(hit, r, w[i])
        n[i] = jnp.where(hit, p, -m * p)
    return w, n


def diag_block(tiles):
    sub = lax.broadcasted_iota(jnp.int32, (8, 128), 0)
    lane = lax.broadcasted_iota(jnp.int32, (8, 128), 1)
    c = list(tiles)
    u, z = [None] * 16, [None] * 16
    e = [lane_col(c[0], k) for k in range(8)]
    for b in range(16):
        s = 8 * b
        here = (lane >= s) & (lane < s + 8)
        h = {t: [lane_col(c[t], s + m) for m in range(8)] for t in range(b + 1, 16)}
        if b < 15:
            old = [lane_col(c[b + 1], s + 8 + k) for k in range(8)]
        w, g = eliminate(e, sub)
        if b < 15:
            hn = h[b + 1]
            gc = [tree(sub_row(g[j], m) * hn[j] for j in range(8)) for m in range(8)]
            e = [
                old[k] - tree(hn[m] * sub_row(gc[m], k) for m in range(8))
                for k in range(8)
            ]
        own = c[b]
        aug = jnp.where(here, jnp.where(lane == s + sub, 1.0, 0.0), own)
        rows = [sub_row(own, k) for k in range(8)]
        rows_aug = [sub_row(aug, k) for k in range(8)]
        u[b] = jnp.where(
            lane >= s + sub, tree(w[k] * rows[k] for k in range(8)), 0.0
        )
        z[b] = jnp.where(lane < s + 8, tree(w[k] * rows_aug[k] for k in range(8)), 0.0)
        scaled = tree(g[k] * rows_aug[k] for k in range(8))
        spread = [sub_row(scaled, m) for m in range(8)]
        for t in range(b + 1, 16):
            c[t] = jnp.where(here, 0.0, c[t]) - tree(
                h[t][m] * spread[m] for m in range(8)
            )
    return jnp.concatenate(u, 0), jnp.concatenate(z, 0)


def place():
    s = lax.axis_index("scen")
    return s % 2, (s // 2) % Z, s // (2 * Z)


def scen_of(core, z, x):
    return {"scen": (x * Z + z) * 2 + core}


def remote(src, dst, send, recv, to):
    return pltpu.make_async_remote_copy(
        src_ref=src, dst_ref=dst, send_sem=send, recv_sem=recv,
        device_id=to, device_id_type=MESH,
    )


def sum_kernel(
    rows, nodes, count, link, inverse, diag, ft, s_out, f_out,
    acc, sib, mine, peer, rm, rp, one_s, one_r, ring_s, ring_r,
):
    core, z, x = place()
    group = lax.axis_index("node")
    down, up = scen_of(core, (z + Z - 1) % Z, x), scen_of(core, (z + 1) % Z, x)
    twin, across = scen_of(1 - core, z, x), scen_of(core, z, 1 - x)
    barrier = pltpu.get_barrier_semaphore()
    for to in (down, up, twin, across):
        pl.semaphore_signal(barrier, inc=1, device_id=to, device_id_type=MESH)
    pl.semaphore_wait(barrier, 4)

    sent = []

    def go(src, dst, send, recv, to):
        copy = remote(src, dst, send, recv, to)
        copy.start()
        sent.append(copy)
        return copy

    f_own = f_out.at[x, z, pl.ds(core * 8, 8), :]
    f_twin = go(ft.at[1 - core], f_own, one_s.at[0], one_r.at[0], twin)
    f_out[x, z, pl.ds(core * 8, 8), :] = ft[core]

    acc[...] = jnp.zeros_like(acc)
    row_id = lax.broadcasted_iota(jnp.int32, (link.shape[1], 1), 0)

    def slot(i, carry):
        limit = jnp.where(i < count[0], rows[i], 0)
        masked = jnp.where(row_id < limit, link[i], 0.0)
        first = nodes[i] == 2 * group
        m = split(masked)
        y = split(mm(split(inverse[i]), m, NN))
        for q in range(K):
            lo = 128 * q
            term = mm(
                (m[0][:, lo : lo + 128], m[1][:, lo : lo + 128]),
                (y[0][:, lo:], y[1][:, lo:]),
                TN,
            )
            for n in range(2):
                part = jnp.where(first, term, 0.0) if n == 0 else jnp.where(first, 0.0, term)
                for j in range(K - q):
                    acc[n, :, OFF[q] + j] += part[:, 128 * j : 128 * j + 128].reshape(
                        16, 8, 128
                    )
        return carry

    lax.fori_loop(0, link.shape[0], slot, 0)
    twin_sum = go(acc.at[1 - core], sib, one_s.at[1], one_r.at[1], twin)
    f_twin.wait_recv()
    f_across = go(f_out.at[x, z], f_out.at[x, z], one_s.at[2], one_r.at[2], across)
    twin_sum.wait_recv()
    acc[core] += sib[...]
    f_across.wait_recv()

    rs_m, rs_p, f_m, f_p = [], [], [], []
    for t in range(8):
        owner = (z + 8 + t) % Z
        if t == 0:
            src = acc.at[core, owner]
        else:
            rs_m[-1].wait_recv()
            rm[t - 1] += acc[core, owner]
            src = rm.at[t - 1]
        rs_m.append(go(src, rm.at[t], ring_s.at[0, t], ring_r.at[0, t], down))
        if t < 7:
            owner = (z + 7 - t) % Z
            if t == 0:
                src = acc.at[core, owner]
            else:
                rs_p[-1].wait_recv()
                rp[t - 1] += acc[core, owner]
                src = rp.at[t - 1]
            rs_p.append(go(src, rp.at[t], ring_s.at[1, t], ring_r.at[1, t], up))
        if t > 0:
            f_m[-1].wait_recv()
        piece = f_out.at[:, (z + t) % Z]
        f_m.append(go(piece, piece, ring_s.at[2, t], ring_r.at[2, t], down))
        if t < 7:
            if t > 0:
                f_p[-1].wait_recv()
            piece = f_out.at[:, (z + Z - t) % Z]
            f_p.append(go(piece, piece, ring_s.at[3, t], ring_r.at[3, t], up))
    rs_m[-1].wait_recv()
    rs_p[-1].wait_recv()
    mine[...] = acc[core, z] + (rm[7] + rp[6])
    swap = go(mine, peer, one_s.at[3], one_r.at[3], across)
    swap.wait_recv()
    sub = lax.broadcasted_iota(jnp.int32, (8, 128), 0)
    lane = lax.broadcasted_iota(jnp.int32, (8, 128), 1)
    s_out[z] = mine[...] + peer[...]
    for q in range(K):
        d = diag[:, 128 * q : 128 * q + 128]
        d = jnp.where(core == 0, d[0:1], d[1:2])
        s_out[z, OFF[q]] += jnp.where(lane == 8 * z + sub, jnp.broadcast_to(d, (8, 128)), 0.0)

    ag_m, ag_p = [], []
    for t in range(8):
        if t > 0:
            ag_m[-1].wait_recv()
        piece = s_out.at[(z + t) % Z]
        ag_m.append(go(piece, piece, ring_s.at[4, t], ring_r.at[4, t], down))
        if t < 7:
            if t > 0:
                ag_p[-1].wait_recv()
            piece = s_out.at[(z + Z - t) % Z]
            ag_p.append(go(piece, piece, ring_s.at[5, t], ring_r.at[5, t], up))
    for last in (ag_m, ag_p, f_m, f_p):
        last[-1].wait_recv()
    for copy in sent:
        copy.wait_send()


def factor_kernel(s_ref, f_ref, g_ref, l_ref, a, xt, low):
    core, z, x = place()
    own = pl.multiple_of((x * Z + z) * 16, 16)

    def block(i, j, q):
        if q == 0:
            return s_ref[:, OFF[i] + j - i].reshape(128, 128)
        return a[i, j]

    low[...] = jnp.zeros_like(low)
    for q in range(K):
        lo = 128 * q
        d = block(q, q, q)
        u, inv = diag_block([d[8 * t : 8 * t + 8, :] for t in range(16)])
        low[lo : lo + 128, lo : lo + 128] = u.T
        inv = split(inv)
        us = {}
        for j in range(q + 1, K):
            v = mm(inv, split(block(q, j, q)), NN)
            low[128 * j : 128 * j + 128, lo : lo + 128] = v.T
            us[j] = split(v)
        for i in range(q + 1, K):
            for j in range(i, K):
                a[i, j] = block(i, j, q) - mm(us[i], us[j], TN)
        src = f_ref if q == 0 else xt
        xq = mm(split(src[:, lo : lo + 128]), inv, NT)
        xt[:, lo : lo + 128] = xq
        xs = split(xq)
        for j in range(q + 1, K):
            hi = 128 * j
            xt[:, hi : hi + 128] = src[:, hi : hi + 128] - mm(xs, us[j], NN)
    g_ref[...] = mm(split(xt[pl.ds(own, 16), :]), split(xt[...]), NT).reshape(2, 8, -1)
    l_ref[...] = low[pl.ds(own, 16), :].reshape(2, 8, -1)


def share_kernel(groups, g_ref, l_ref, fd, l_out, first_out, got, send, recv, ls, lr):
    core, z, x = place()
    group = lax.axis_index("node")
    scen = lax.axis_index("scen")
    barrier = pltpu.get_barrier_semaphore()
    peers = []
    for c in range(2):
        for n in range(groups):
            if c == 0 and n == 0:
                continue
            to_core = (core + c) % 2
            to_node = (group + n) % groups
            peers.append(
                (to_core, to_node, {"scen": (x * Z + z) * 2 + to_core, "node": to_node})
            )
    for _, _, to in peers:
        pl.semaphore_signal(barrier, inc=1, device_id=to, device_id_type=MESH)
    pl.semaphore_wait(barrier, len(peers))
    copies = []
    for i, (to_core, _, to) in enumerate(peers):
        copies.append(
            remote(g_ref.at[to_core], got.at[core, group], send.at[i], recv.at[i], to)
        )
    twin = {"scen": (x * Z + z) * 2 + 1 - core}
    copies.append(remote(l_ref.at[1 - core], l_out.at[core], ls, lr, twin))
    for copy in copies:
        copy.start()
    l_out[core] = l_ref[core]
    got[core, group] = g_ref[core]
    for copy in copies:
        copy.wait()
    width = first_out.shape[1]
    sub = lax.broadcasted_iota(jnp.int32, (8, width), 0)
    lane = lax.broadcasted_iota(jnp.int32, (8, width), 1)
    total = tree(got[c, n] for c in range(2) for n in range(groups))
    first_out[...] = total + jnp.where(lane == scen * 8 + sub, fd[...], 0.0)


def shards(
    link_blocks, inverse_blocks, block_rows, node_of, slot_count, node_diag, first_link, first_diag
):
    groups = lax.axis_size("node")
    width = link_blocks.shape[2]
    ft = jnp.swapaxes(first_link, 1, 2)
    fd = jnp.broadcast_to(first_diag[:, None], (8, width))
    vmem = pl.BlockSpec(memory_space=pltpu.VMEM)
    smem = pl.BlockSpec(memory_space=pltpu.SMEM)
    dma = pltpu.SemaphoreType.DMA
    chunk = (TILES, 8, 128)
    s_all, f_all = pl.pallas_call(
        sum_kernel,
        out_shape=[
            jax.ShapeDtypeStruct((Z, *chunk), f32),
            jax.ShapeDtypeStruct((2, Z, 16, width), f32),
        ],
        in_specs=[smem] * 3 + [vmem] * 4,
        out_specs=[vmem] * 2,
        scratch_shapes=[
            pltpu.VMEM((2, Z, *chunk), f32),
            pltpu.VMEM((Z, *chunk), f32),
            pltpu.VMEM(chunk, f32),
            pltpu.VMEM(chunk, f32),
            pltpu.VMEM((8, *chunk), f32),
            pltpu.VMEM((7, *chunk), f32),
            dma((4,)),
            dma((4,)),
            dma((6, 8)),
            dma((6, 8)),
        ],
        compiler_params=pltpu.CompilerParams(
            collective_id=0, has_side_effects=True, vmem_limit_bytes=40 << 20
        ),
        name="sum_kernel",
    )(block_rows, node_of, slot_count, link_blocks, inverse_blocks, node_diag, ft)
    g_own, l_own = pl.pallas_call(
        factor_kernel,
        out_shape=[jax.ShapeDtypeStruct((2, 8, width), f32)] * 2,
        in_specs=[vmem] * 2,
        out_specs=[vmem] * 2,
        scratch_shapes=[
            pltpu.VMEM((K, K, 128, 128), f32),
            pltpu.VMEM((width, width), f32),
            pltpu.VMEM((width, width), f32),
        ],
        compiler_params=pltpu.CompilerParams(vmem_limit_bytes=40 << 20),
        name="factor_kernel",
    )(s_all, f_all.reshape(2 * Z * 16, width))
    node_factor, first_schur = pl.pallas_call(
        functools.partial(share_kernel, groups),
        out_shape=[
            jax.ShapeDtypeStruct((2, 8, width), f32),
            jax.ShapeDtypeStruct((8, width), f32),
        ],
        in_specs=[vmem] * 3,
        out_specs=[vmem] * 2,
        scratch_shapes=[
            pltpu.VMEM((2, groups, 8, width), f32),
            dma((2 * groups - 1,)),
            dma((2 * groups - 1,)),
            dma(()),
            dma(()),
        ],
        compiler_params=pltpu.CompilerParams(collective_id=1, has_side_effects=True),
        name="share_kernel",
    )(g_own, l_own, fd)
    return (node_factor, first_schur)


def solution(mesh):
    in_specs = (
        P(("scen", "node"), None, None),
        P(("scen", "node"), None, None),
        P(("scen", "node")),
        P(("scen", "node")),
        P(("scen", "node")),
        P("node", None),
        P("node", None, "scen"),
        P("scen"),
    )
    out_specs = (P("node", "scen", None), P("scen", None))
    return jax.shard_map(shards, mesh=mesh, in_specs=in_specs, out_specs=out_specs, check_vma=False)
```

time: 1210 us -> 114 us (0.09)
  waiting for transfers between devices: 858 us -> 0 us
  other arithmetic: 242 us -> 0 us
  Pallas kernels: 0 us -> 102 us
  local copies, waits for them, and re-layouts: 39.9 us -> 10.2 us
  blocking collectives: 26.3 us -> 0 us
  matrix products: 17.9 us -> 0 us
  between operations: 14.9 us -> 1.31 us
    unnamed x4 -> x0, waiting for transfers between devices: 581 us -> none
    all_gather x2 -> x0, waiting for transfers between devices: 277 us -> none  [the longest x1 140 us: shards(): gathered = lax.all_gather(row_terms, 'scen', axis=1, tiled=True)]
    another operation x20 -> x0, other arithmetic: 237 us -> none  [the longest x16 154 us: shards(): factor = jnp.linalg.cholesky(gathered + node_diag[:, :, None] * identity)]
    pallas_call x0 -> x3, Pallas kernels: none -> 102 us  [the longest x1 64.9 us: shards(): pl.pallas_call(sum_kernel, out_shape=[jax.ShapeDtypeStruct((Z, *chunk), f...]
    psum x1 -> x0, blocking collectives: 26.3 us -> none  [shards(): summed = lax.psum(row_block, 'node')]
    another operation x17 -> x0, local copies, waits for them, and re-layouts: 14.3 us -> none
  transfers between devices with their start and end apart: 3 -> 0, of which waited for: 3 -> 0; matrix products, arithmetic and copies ran while one was open for 0% -> 0% of each run, Pallas kernels for 0% -> 0%
where the time goes in v1:
time: 114 us
  Pallas kernels  102 us (89%)
  local copies, waits for them, and re-layouts  10.2 us (9%)
  between operations  1.31 us (1%)
    pallas_call x1, Pallas kernels, shards(): pl.pallas_call(sum_kernel, out_shape=[jax.ShapeDtypeStruct((Z, *chunk), f...  64.9 us
    pallas_call x1, Pallas kernels, shards(): pl.pallas_call(functools.partial(share_kernel, groups), out_shape=[jax.Sh...  23.3 us
    pallas_call x1, Pallas kernels, shards(): pl.pallas_call(factor_kernel, out_shape=[jax.ShapeDtypeStruct((2, 8, widt...  13.9 us
    unnamed x20, local copies, waits for them, and re-layouts  9.5 us

profile of v1, /device:TPU:1, one launch (start us, length us, event | category | flops | bytes accessed | tf_op | source)
XLA Modules:
  0.0 113.6 jit_solution(1225435452892430430)
XLA Ops:
  1.3 0.0 copy-start
  1.3 1.6 %copy-done = f32[4,256,512]{2,1,0:T(8,128)S(1)} copy-done((f32[4,256,512]{2,1,0:T(8,128)S(1)}, f32[4,256,512]{2,1,0:T(8,128)}, u32[]{:S(2)}) %copy-start) | copy-done | bytes 2097176
  2.9 0.0 copy-start.1
  2.9 1.2 %copy-done.1 = f32[4,256,256]{2,1,0:T(8,128)S(1)} copy-done((f32[4,256,256]{2,1,0:T(8,128)S(1)}, f32[4,256,256]{2,1,0:T(8,128)}, u32[]{:S(2)}) %copy-start.1) | copy-done | bytes 1048600
  4.1 0.0 copy-start.2
  4.1 0.8 copy-done.2
  4.9 0.0 copy-start.5
  4.9 0.7 copy-done.5
  5.5 0.0 copy-start.6
  5.5 0.7 copy-done.6
  6.2 0.0 copy-start.7
  6.2 0.7 copy-done.7
  6.9 0.0 copy-start.8
  6.9 64.9 %sum_kernel.1 = (f32[16,10,8,128]{3,2,1,0:T(8,128)S(1)}, f32[2,16,16,512]{3,2,1,0:T(8,128)S(1)}) custom-call(s32[4]{0:T(128)S(1)} %copy-done.6, s32[4]{0:T(128)S(1)} %copy-done.7, s32[1]{0:T(128)S(6)} %copy.12.count, f32[4,256,512]{2,1,0:T(8,128)S(1)} %copy-done, f32[4,256,256]{2,1,0:T(8,128)S(1)} %copy-done.1, f32[2,512]{1,0:T(2,128)S(1)} %copy-done.5, ...), custom_call_target="tpu_custom_call" | custom-call | tf_op jit(solution)/shard_map/sum_kernel/pallas_call | solution.py:324
  71.8 13.9 %factor_kernel.1 = (f32[2,8,512]{2,1,0:T(8,128)S(1)}, f32[2,8,512]{2,1,0:T(8,128)S(1)}) custom-call(f32[16,10,8,128]{3,2,1,0:T(8,128)S(1)} %get-tuple-element.6.s_ref, f32[512,512]{1,0:T(8,128)S(1)} %bitcast.2), custom_call_target="tpu_custom_call" | custom-call | tf_op jit(solution)/shard_map/factor_kernel/pallas_call | solution.py:349
  85.7 0.0 copy-start.3
  85.7 0.6 copy-done.3
  86.3 0.0 copy-start.4
  86.3 0.6 copy-done.4
  86.9 0.0 copy-done.8
  86.9 0.7 broadcast_in_dim.2.fd
  87.6 23.3 %share_kernel.1 = (f32[2,8,512]{2,1,0:T(8,128)}, f32[8,512]{1,0:T(8,128)}) custom-call(f32[2,8,512]{2,1,0:T(8,128)} %copy-done.3, f32[2,8,512]{2,1,0:T(8,128)} %copy-done.4, f32[8,512]{1,0:T(8,128)} %broadcast_in_dim.2.fd), custom_call_target="tpu_custom_call" | custom-call | tf_op jit(solution)/shard_map/share_kernel/pallas_call | solution.py:362
  110.9 1.4 %copy.13 = f32[2,8,512]{2,1,0:T(8,128)} copy(f32[2,8,512]{2,1,0:T(8,128)} %get-tuple-element.12) | data formatting | bytes 65536
  112.2 1.3 %copy.14 = f32[8,512]{1,0:T(8,128)} copy(f32[8,512]{1,0:T(8,128)} %get-tuple-element.13) | data formatting | bytes 32768
Async XLA Ops:
  1.3 1.6 %copy-start = (f32[4,256,512]{2,1,0:T(8,128)S(1)}, f32[4,256,512]{2,1,0:T(8,128)}, u32[]{:S(2)}) copy-start(f32[4,256,512]{2,1,0:T(8,128)} %link.1) | copy-start | bytes 6291460
  2.9 1.2 %copy-start.1 = (f32[4,256,256]{2,1,0:T(8,128)S(1)}, f32[4,256,256]{2,1,0:T(8,128)}, u32[]{:S(2)}) copy-start(f32[4,256,256]{2,1,0:T(8,128)} %inverse.1) | copy-start | bytes 3145732
  4.1 0.8 copy-start.2
  4.9 0.7 copy-start.5
  5.5 0.7 copy-start.6
  6.2 0.7 copy-start.7
  6.9 80.0 %copy-start.8 = (f32[8]{0:T(128)S(1)}, f32[8]{0:T(128)}, u32[]{:S(2)}) copy-start(f32[8]{0:T(128)} %param.15) | copy-start | bytes 100
  85.7 0.6 copy-start.3
  86.3 0.6 copy-start.4

commit v2 on v0

v2 whole, which is shorter than its diff:
```python
import functools

import jax
import jax.numpy as jnp
from jax import lax
from jax.experimental import pallas as pl
from jax.experimental.pallas import tpu as pltpu
from jax.sharding import PartitionSpec as P

f32, bf16 = jnp.float32, jnp.bfloat16
NN = (((1,), (0,)), ((), ()))
NT = (((1,), (1,)), ((), ()))
TN = (((0,), (0,)), ((), ()))
Z = 16
K = 4
WAVES = (
    ((0, 0),),
    ((0, 1), (0, 2), (0, 3)),
    ((1, 1), (1, 2), (1, 3)),
    ((2, 2), (2, 3), (3, 3)),
)
WAVE_OF = {block: (w, i) for w, wave in enumerate(WAVES) for i, block in enumerate(wave)}
FAR_FIRST = (8, 7, 9, 6, 10, 5, 11, 4, 12, 3, 13, 2, 14, 1, 15)
MESH = pl.DeviceIdType.MESH


def split(x):
    high = x.astype(bf16)
    return high, (x - high.astype(f32)).astype(bf16)


def mm(a, b, dims):
    def one(p, q):
        return lax.dot_general(p, q, dims, preferred_element_type=f32)

    return one(a[0], b[0]) + (one(a[0], b[1]) + one(a[1], b[0]))


def sub_row(x, k):
    return jnp.broadcast_to(x[k : k + 1, :], (8, 128))


def lane_col(x, j):
    return jnp.broadcast_to(x[:, j : j + 1], x.shape)


def stack(parts):
    return jnp.concatenate([x[None] for x in parts], 0)


def tree(terms):
    terms = list(terms)
    while len(terms) > 1:
        terms = [
            terms[i] + terms[i + 1] if i + 1 < len(terms) else terms[i]
            for i in range(0, len(terms), 2)
        ]
    return terms[0]


def eliminate(n, hit):
    w = None
    for i in range(8):
        row = jnp.broadcast_to(n[:, i : i + 1, :], (8, 8, 128))
        p = 1.0 / row[i]
        r = lax.rsqrt(row[i])
        m = jnp.where(hit[i], 0.0, n[i])
        c = row * p
        new = jnp.where(hit[i], c, n - m * c)
        parts = [new[:i]] if i else []
        parts.append(jnp.where(hit[i], p, -m * p)[None])
        if i < 7:
            parts.append(new[i + 1 :])
        n = jnp.concatenate(parts, 0)
        mine = jnp.where(hit[i], r, 0.0)[None]
        if i:
            mine = jnp.concatenate([jnp.where(hit[i], row[:i] * r, w), mine], 0)
        w = mine
    return w, n


def diag_block(c):
    sub = lax.broadcasted_iota(jnp.int32, (8, 128), 0)
    lane = lax.broadcasted_iota(jnp.int32, (8, 128), 1)
    hit = [sub == i for i in range(8)]
    u, z = [], []
    e = stack([lane_col(c[0:8], k) for k in range(8)])
    for b in range(16):
        s, rest = 8 * b, 120 - 8 * b
        here = (lane >= s) & (lane < s + 8)
        own = c[:8]
        if rest:
            c = c[8:]
            h = [lane_col(c, s + m) for m in range(8)]
            old = [lane_col(c[:8], s + 8 + k) for k in range(8)]
        w, g = eliminate(e, hit)
        if rest:
            hn = [x[:8] for x in h]
            gc = tree(jnp.broadcast_to(g[:, j : j + 1, :], (8, 8, 128)) * hn[j] for j in range(8))
            e = stack(
                [old[k] - tree(hn[m] * sub_row(gc[m], k) for m in range(8)) for k in range(8)]
            )
        aug = jnp.where(here, jnp.where(lane == s + sub, 1.0, 0.0), own)
        rows = [sub_row(aug, k) for k in range(8)]
        u.append(
            jnp.where(lane >= s + sub, tree(w[k] * sub_row(own, k) for k in range(8)), 0.0)
        )
        z.append(jnp.where(lane < s + 8, tree(w[k] * rows[k] for k in range(8)), 0.0))
        if rest:
            scaled = tree(g[k] * rows[k] for k in range(8))
            wide = lax.broadcasted_iota(jnp.int32, (rest, 128), 1)
            c = jnp.where((wide >= s) & (wide < s + 8), 0.0, c) - tree(
                h[m] * jnp.broadcast_to(scaled[m : m + 1], (rest, 128)) for m in range(8)
            )
    return jnp.concatenate(u, 0), jnp.concatenate(z, 0)


def remote(src, dst, send, recv, to):
    return pltpu.make_async_remote_copy(
        src_ref=src, dst_ref=dst, send_sem=send, recv_sem=recv,
        device_id=to, device_id_type=MESH,
    )


def kernel(
    groups, rows, nodes, count, fd, link_hbm, inverse_hbm, diag, ft, l_out, first_out,
    link, inverse, f_all, a, xt, low, g_own, got, load, one_s, one_r,
    f_s, f_r, f2_s, f2_r, end_s, end_r, *wave_refs,
):
    scen = lax.axis_index("scen")
    core, z, x = scen % 2, (scen // 2) % Z, scen // (2 * Z)
    group = lax.axis_index("node")

    def chip(dz):
        return {"scen": (x * Z + (z + dz) % Z) * 2 + core}

    twin = {"scen": scen + 1 - 2 * core}
    across = {"scen": ((1 - x) * Z + z) * 2 + core}
    finals = []
    for c in range(2):
        for n in range(groups):
            if c + n > 0:
                to_core = (core + c) % 2
                to = {"scen": scen - core + to_core, "node": (group + n) % groups}
                finals.append((to_core, to))
    barrier = pltpu.get_barrier_semaphore()
    greet = [chip(d) for d in range(1, Z)] + [across] + [to for _, to in finals]
    for to in greet:
        pl.semaphore_signal(barrier, inc=1, device_id=to, device_id_type=MESH)

    slots = link.shape[0]
    loads = []
    for i in range(slots):
        for n, (src, dst) in enumerate(((link_hbm, link), (inverse_hbm, inverse))):
            loads.append(pltpu.make_async_copy(src.at[i], dst.at[i], load.at[n, i]))
            loads[-1].start()

    waves = []
    per = len(wave_refs) // len(WAVES)
    for w in range(len(WAVES)):
        waves.append(wave_refs[per * w : per * w + per])
    sent = []

    def go(src, dst, send, recv, to):
        copy = remote(src, dst, send, recv, to)
        copy.start()
        sent.append(copy)
        return copy

    for acc, *_ in waves:
        acc[...] = jnp.zeros_like(acc)
    row_id = lax.broadcasted_iota(jnp.int32, (link.shape[1], 1), 0)
    for copy in loads:
        copy.wait()

    def slot(i, carry):
        limit = jnp.where(i < count[0], rows[i], 0)
        masked = jnp.where(row_id < limit, link[i], 0.0)
        first = nodes[i] == 2 * group
        m = split(masked)
        y = split(mm(split(inverse[i]), m, NN))
        for q in range(K):
            lo = 128 * q
            term = mm(
                (m[0][:, lo : lo + 128], m[1][:, lo : lo + 128]),
                (y[0][:, lo:], y[1][:, lo:]),
                TN,
            )
            for j in range(K - q):
                w, p = WAVE_OF[q, q + j]
                acc = waves[w][0]
                part = term[:, 128 * j : 128 * j + 128].reshape(16, 8, 128)
                acc[0, :, p] += jnp.where(first, part, 0.0)
                acc[1, :, p] += jnp.where(first, 0.0, part)
        return carry

    lax.fori_loop(0, slots, slot, 0)
    pl.semaphore_wait(barrier, len(greet))

    twins = []
    for w, (acc, sib, *_) in enumerate(waves):
        twins.append(go(acc.at[1 - core], sib, one_s.at[0, w], one_r.at[0, w], twin))
        if w == 0:
            f_own = f_all.at[x, z, pl.ds(core * 8, 8), :]
            f_twin = go(ft.at[1 - core], f_own, f_s.at[0], f_r.at[0], twin)
    f_all[x, z, pl.ds(core * 8, 8), :] = ft[core]

    parts = []
    for w, (acc, sib, rs, mine, peer, s_all, rs_s, rs_r, ag_s, ag_r) in enumerate(waves):
        twins[w].wait_recv()
        acc[core] += sib[...]
        parts.append(
            [
                go(acc.at[core, (z + d) % Z], rs.at[z], rs_s.at[d - 1], rs_r.at[d - 1], chip(d))
                for d in FAR_FIRST
            ]
        )
        rs[z] = acc[core, z]
        if w == 0:
            f_twin.wait_recv()
            f_across = go(f_all.at[x, z], f_all.at[x, z], f_s.at[1], f_r.at[1], across)

    f_across.wait_recv()
    piece = f_all.at[:, z]
    f_far = [
        go(piece, piece, f_s.at[2 + i], f_r.at[2 + i], chip(d)) for i, d in enumerate((8, 4, 12))
    ]

    def swap(w):
        acc, sib, rs, mine, peer, *_ = waves[w]
        for copy in parts[w]:
            copy.wait_recv()
        mine[...] = tree(rs[i] for i in range(Z))
        return go(mine, peer, one_s.at[1, w], one_r.at[1, w], across)

    sub = lax.broadcasted_iota(jnp.int32, (8, 128), 0)
    lane = lax.broadcasted_iota(jnp.int32, (8, 128), 1)

    def spread(w, swapped):
        acc, sib, rs, mine, peer, s_all, rs_s, rs_r, ag_s, ag_r = waves[w]
        swapped.wait_recv()
        s_all[z] = mine[...] + peer[...]
        for q in range(K):
            if WAVE_OF[q, q][0] == w:
                d = diag[:, 128 * q : 128 * q + 128]
                d = jnp.broadcast_to(jnp.where(core == 0, d[0:1], d[1:2]), (8, 128))
                s_all[z, WAVE_OF[q, q][1]] += jnp.where(lane == 8 * z + sub, d, 0.0)
        return [
            go(s_all.at[z], s_all.at[z], ag_s.at[d - 1], ag_r.at[d - 1], chip(d))
            for d in FAR_FIRST
        ]

    swap0 = swap(0)
    swap1 = swap(1)
    gather0 = spread(0, swap0)
    swap2 = swap(2)
    gather1 = spread(1, swap1)
    for copy in f_far:
        copy.wait_recv()
    f_near = []
    for i, d in enumerate((15, 1, 2)):
        for k in range(4):
            piece = f_all.at[:, (z + 4 * k) % Z]
            f_near.append(go(piece, piece, f2_s.at[i, k], f2_r.at[i, k], chip(d)))
    swap3 = swap(3)
    gather2 = spread(2, swap2)
    gather3 = spread(3, swap3)
    gathers = (gather0, gather1, gather2, gather3)

    def arrive(copies):
        for copy in copies:
            copy.wait_recv()

    def block(i, j):
        w, p = WAVE_OF[i, j]
        return waves[w][5][:, p].reshape(128, 128)

    low[...] = jnp.zeros_like(low)
    us, invs = {}, []

    def solve(q):
        lo = 128 * q
        src = xt
        if q == 0:
            part = f_all[...].reshape(4 * 128, -1)[:, lo : lo + 128]
        else:
            part = xt[:, lo : lo + 128]
        xq = mm(split(part), invs[q], NT)
        xs = split(xq)
        for j in range(q + 1, K):
            hi = 128 * j
            old = f_all[...].reshape(4 * 128, -1)[:, hi : hi + 128] if q == 0 else xt[:, hi : hi + 128]
            xt[:, hi : hi + 128] = old - mm(xs, us[q, j], NN)
        xt[:, lo : lo + 128] = xq

    arrive(gather0)
    for q in range(K):
        lo = 128 * q
        u, inv = diag_block(block(0, 0) if q == 0 else a[q, q])
        low[lo : lo + 128, lo : lo + 128] = u.T
        invs.append(split(inv))
        if q == 0:
            arrive(gather1)
        for j in range(q + 1, K):
            v = mm(invs[q], split(block(0, j) if q == 0 else a[q, j]), NN)
            low[128 * j : 128 * j + 128, lo : lo + 128] = v.T
            us[q, j] = split(v)
        if q == 0:
            arrive(gather2)
            for j in range(1, K):
                a[1, j] = block(1, j) - mm(us[0, 1], us[0, j], TN)
        elif q == 1:
            arrive(gather3)
            arrive(f_near)
            for i in range(2, K):
                for j in range(i, K):
                    a[i, j] = block(i, j) - (
                        mm(us[0, i], us[0, j], TN) + mm(us[1, i], us[1, j], TN)
                    )
            solve(0)
            solve(1)
        elif q == 2:
            a[3, 3] -= mm(us[2, 3], us[2, 3], TN)
            solve(2)
        else:
            solve(3)

    own = pl.multiple_of((x * Z + z) * 16, 16)
    width = first_out.shape[1]
    g_own[0] = low[pl.ds(own, 8), :]
    g_own[1] = low[pl.ds(pl.multiple_of(own + 8, 8), 8), :]
    factor = go(g_own.at[1 - core], l_out.at[core], end_s.at[0], end_r.at[0], twin)
    l_out[core] = g_own[core]
    term = mm(split(xt[pl.ds(own, 16), :]), split(xt[...]), NT)
    g_own[2] = term[:8]
    g_own[3] = term[8:]
    last = [
        go(g_own.at[2 + to_core], got.at[core, group], end_s.at[1 + i], end_r.at[1 + i], to)
        for i, (to_core, to) in enumerate(finals)
    ]
    got[core, group] = g_own[2 + core]
    arrive(last)
    row8 = lax.broadcasted_iota(jnp.int32, (8, width), 0)
    col8 = lax.broadcasted_iota(jnp.int32, (8, width), 1)
    d = jnp.zeros((8, width), f32)
    for i in range(8):
        d = jnp.where(row8 == i, fd[i], d)
    total = tree(got[c, n] for c in range(2) for n in range(groups))
    first_out[...] = total + jnp.where(col8 == scen * 8 + row8, d, 0.0)
    factor.wait_recv()
    for copy in sent:
        copy.wait_send()


def shards(
    link_blocks, inverse_blocks, block_rows, node_of, slot_count, node_diag, first_link, first_diag
):
    groups = lax.axis_size("node")
    width = link_blocks.shape[2]
    ft = jnp.swapaxes(first_link, 1, 2)
    vmem = pl.BlockSpec(memory_space=pltpu.VMEM)
    smem = pl.BlockSpec(memory_space=pltpu.SMEM)
    hbm = pl.BlockSpec(memory_space=pl.ANY)
    dma = pltpu.SemaphoreType.DMA
    waves = []
    for wave in WAVES:
        tile = (len(wave), 8, 128)
        waves += [
            pltpu.VMEM((2, Z, *tile), f32),
            pltpu.VMEM((Z, *tile), f32),
            pltpu.VMEM((Z, *tile), f32),
            pltpu.VMEM(tile, f32),
            pltpu.VMEM(tile, f32),
            pltpu.VMEM((Z, *tile), f32),
        ] + [dma((Z - 1,))] * 4
    return pl.pallas_call(
        functools.partial(kernel, groups),
        out_shape=[
            jax.ShapeDtypeStruct((2, 8, width), f32),
            jax.ShapeDtypeStruct((8, width), f32),
        ],
        in_specs=[smem] * 4 + [hbm] * 2 + [vmem] * 2,
        out_specs=[vmem] * 2,
        scratch_shapes=[
            pltpu.VMEM(link_blocks.shape, f32),
            pltpu.VMEM(inverse_blocks.shape, f32),
            pltpu.VMEM((2, Z, 16, width), f32),
            pltpu.VMEM((K, K, 128, 128), f32),
            pltpu.VMEM((width, width), f32),
            pltpu.VMEM((width, width), f32),
            pltpu.VMEM((4, 8, width), f32),
            pltpu.VMEM((2, groups, 8, width), f32),
            dma((2, link_blocks.shape[0])),
            dma((2, len(WAVES))),
            dma((2, len(WAVES))),
            dma((5,)),
            dma((5,)),
            dma((3, 4)),
            dma((3, 4)),
            dma((2 * groups,)),
            dma((2 * groups,)),
            *waves,
        ],
        compiler_params=pltpu.CompilerParams(
            collective_id=0, has_side_effects=True, vmem_limit_bytes=50 << 20
        ),
        name="schur",
    )(
        block_rows, node_of, slot_count, first_diag,
        link_blocks, inverse_blocks, node_diag, ft,
    )


def solution(mesh):
    in_specs = (
        P(("scen", "node"), None, None),
        P(("scen", "node"), None, None),
        P(("scen", "node")),
        P(("scen", "node")),
        P(("scen", "node")),
        P("node", None),
        P("node", None, "scen"),
        P("scen"),
    )
    out_specs = (P("node", "scen", None), P("scen", None))
    return jax.shard_map(shards, mesh=mesh, in_specs=in_specs, out_specs=out_specs, check_vma=False)
```

time: 1210 us -> 130 us (0.11)
  waiting for transfers between devices: 858 us -> 0 us
  other arithmetic: 242 us -> 0 us
  Pallas kernels: 0 us -> 121 us
  local copies, waits for them, and re-layouts: 39.9 us -> 7.44 us
  blocking collectives: 26.3 us -> 0 us
  matrix products: 17.9 us -> 0 us
  between operations: 14.9 us -> 1.3 us
    unnamed x4 -> x0, waiting for transfers between devices: 581 us -> none
    all_gather x2 -> x0, waiting for transfers between devices: 277 us -> none  [the longest x1 140 us: shards(): gathered = lax.all_gather(row_terms, 'scen', axis=1, tiled=True)]
    another operation x20 -> x0, other arithmetic: 237 us -> none  [the longest x16 154 us: shards(): factor = jnp.linalg.cholesky(gathered + node_diag[:, :, None] * identity)]
    pallas_call x0 -> x1, Pallas kernels: none -> 121 us  [shards(): pl.pallas_call(functools.partial(kernel, groups), out_shape=[jax.ShapeDty...]
    psum x1 -> x0, blocking collectives: 26.3 us -> none  [shards(): summed = lax.psum(row_block, 'node')]
    another operation x17 -> x0, local copies, waits for them, and re-layouts: 14.3 us -> none
  transfers between devices with their start and end apart: 3 -> 0, of which waited for: 3 -> 0; matrix products, arithmetic and copies ran while one was open for 0% -> 0% of each run, Pallas kernels for 0% -> 0%
where the time goes in v2:
time: 130 us
  Pallas kernels  121 us (93%)
  local copies, waits for them, and re-layouts  7.44 us (6%)
  between operations  1.3 us (1%)
    pallas_call x1, Pallas kernels, shards(): pl.pallas_call(functools.partial(kernel, groups), out_shape=[jax.ShapeDty...  121 us
    unnamed x16, local copies, waits for them, and re-layouts  7.44 us

profile of v2, /device:TPU:1, one launch (start us, length us, event | category | flops | bytes accessed | tf_op | source)
XLA Modules:
  0.0 129.9 jit_solution(6060494395939839594)
XLA Ops:
  1.3 0.0 copy-start
  1.3 1.6 %copy-done = f32[4,256,512]{2,1,0:T(8,128)S(1)} copy-done((f32[4,256,512]{2,1,0:T(8,128)S(1)}, f32[4,256,512]{2,1,0:T(8,128)}, u32[]{:S(2)}) %copy-start) | copy-done | bytes 2097176
  2.9 0.0 copy-start.1
  2.9 1.2 copy-done.1
  4.1 0.0 copy-start.2
  4.1 0.8 copy-done.2
  4.9 0.0 copy-start.3
  4.9 0.7 copy-done.3
  5.5 0.0 copy-start.4
  5.5 0.7 copy-done.4
  6.2 0.0 copy-start.5
  6.2 0.7 copy-done.5
  6.9 0.0 copy-start.6
  6.9 0.7 copy-done.6
  7.5 121.1 %schur.1 = (f32[2,8,512]{2,1,0:T(8,128)S(1)}, f32[8,512]{1,0:T(8,128)S(1)}) custom-call(s32[4]{0:T(128)S(1)} %copy-done.4, s32[4]{0:T(128)S(1)} %copy-done.5, s32[1]{0:T(128)S(6)} %copy.12.count, f32[8]{0:T(128)S(1)} %copy-done.6, f32[4,256,512]{2,1,0:T(8,128)S(1)} %copy-done, f32[4,256,256]{2,1,0:T(8,128)S(1)} %copy-done.1, f32[2,512]{1,0:T(2,128)S(1)} %copy-done.3, ...), custom_call_target="tpu_custom_call" | custom-call | tf_op jit(solution)/shard_map/schur/pallas_call | solution.py:376
  128.6 0.6 copy.13
  129.3 0.6 copy.14
Async XLA Ops:
  1.3 1.6 %copy-start = (f32[4,256,512]{2,1,0:T(8,128)S(1)}, f32[4,256,512]{2,1,0:T(8,128)}, u32[]{:S(2)}) copy-start(f32[4,256,512]{2,1,0:T(8,128)} %link_hbm.1) | copy-start | bytes 6291460
  2.9 1.2 copy-start.1
  4.1 0.8 copy-start.2
  4.9 0.7 copy-start.3
  5.5 0.7 copy-start.4
  6.2 0.7 copy-start.5
  6.9 0.7 copy-start.6

commit v3 on v2

--- a/solution.py
+++ b/solution.py
@@ -124,12 +124,15 @@
 
 def kernel(
     groups, rows, nodes, count, fd, link_hbm, inverse_hbm, diag, ft, l_out, first_out,
-    link, inverse, f_all, a, xt, low, g_own, got, load, one_s, one_r,
-    f_s, f_r, f2_s, f2_r, end_s, end_r, *wave_refs,
+    link, inverse, f_all, a, xt, low, g_own, got, load, twin_s, twin_r, swap_s, swap_r,
+    f_s, f_r, end_s, end_r, *wave_refs,
 ):
     scen = lax.axis_index("scen")
     core, z, x = scen % 2, (scen // 2) % Z, scen // (2 * Z)
+    high, kind = z // 4, z % 4
+    strip = 4 * kind + high
     group = lax.axis_index("node")
+    near_by = (1, 15, 2 + 12 * core)
 
     def chip(dz):
         return {"scen": (x * Z + (z + dz) % Z) * 2 + core}
@@ -155,10 +158,8 @@
             loads.append(pltpu.make_async_copy(src.at[i], dst.at[i], load.at[n, i]))
             loads[-1].start()
 
-    waves = []
     per = len(wave_refs) // len(WAVES)
-    for w in range(len(WAVES)):
-        waves.append(wave_refs[per * w : per * w + per])
+    waves = [wave_refs[per * w : per * w + per] for w in range(len(WAVES))]
     sent = []
 
     def go(src, dst, send, recv, to):
@@ -166,6 +167,10 @@
         copy.start()
         sent.append(copy)
         return copy
+
+    def arrive(copies):
+        for copy in copies:
+            copy.wait_recv()
 
     for acc, *_ in waves:
         acc[...] = jnp.zeros_like(acc)
@@ -199,81 +204,102 @@
 
     twins = []
     for w, (acc, sib, *_) in enumerate(waves):
-        twins.append(go(acc.at[1 - core], sib, one_s.at[0, w], one_r.at[0, w], twin))
+        twins.append(go(acc.at[1 - core], sib, twin_s.at[w], twin_r.at[w], twin))
         if w == 0:
-            f_own = f_all.at[x, z, pl.ds(core * 8, 8), :]
+            f_own = f_all.at[x, high, kind, pl.ds(core * 8, 8), :]
             f_twin = go(ft.at[1 - core], f_own, f_s.at[0], f_r.at[0], twin)
-    f_all[x, z, pl.ds(core * 8, 8), :] = ft[core]
-
-    parts = []
-    for w, (acc, sib, rs, mine, peer, s_all, rs_s, rs_r, ag_s, ag_r) in enumerate(waves):
+    f_all[x, high, kind, pl.ds(core * 8, 8), :] = ft[core]
+
+    acc, sib, rs, _, mine0, peer0, s0, s_sem, r_sem = waves[0]
+    twins[0].wait_recv()
+    acc[core] += sib[...]
+    direct = []
+    for d in FAR_FIRST:
+        to = (z + d) % Z
+        direct.append(
+            go(acc.at[core, 4 * (to % 4) + to // 4], rs.at[z], s_sem.at[d], r_sem.at[d], chip(d))
+        )
+    rs[z] = acc[core, strip]
+    f_twin.wait_recv()
+    f_own = f_all.at[x, high, kind]
+    f_across = go(f_own, f_own, f_s.at[1], f_r.at[1], across)
+    near = {}
+    for w in range(1, len(WAVES)):
+        acc, sib, rs, half, mine, peer, s_all, s_sem, r_sem = waves[w]
         twins[w].wait_recv()
         acc[core] += sib[...]
-        parts.append(
-            [
-                go(acc.at[core, (z + d) % Z], rs.at[z], rs_s.at[d - 1], rs_r.at[d - 1], chip(d))
-                for d in FAR_FIRST
-            ]
-        )
-        rs[z] = acc[core, z]
+        near[w] = [
+            go(
+                acc.at[core, pl.ds(4 * ((z + d) % 4), 4)], rs.at[pl.ds(4 * i, 4)],
+                s_sem.at[i], r_sem.at[i], chip(d),
+            )
+            for i, d in enumerate(near_by)
+        ]
+    far = {}
+    for w in range(1, len(WAVES)):
+        acc, sib, rs, half, mine, peer, s_all, s_sem, r_sem = waves[w]
+        arrive(near[w])
+        half[...] = (acc[core, pl.ds(4 * kind, 4)] + rs[0:4]) + (rs[4:8] + rs[8:12])
+        far[w] = [
+            go(half.at[(high + k) % 4], rs.at[11 + k], s_sem.at[2 + k], r_sem.at[2 + k], chip(4 * k))
+            for k in (2, 1, 3)
+        ]
+
+    f_across.wait_recv()
+    piece = f_all.at[:, high, kind]
+    f_far = [go(piece, piece, f_s.at[1 + k], f_r.at[1 + k], chip(4 * k)) for k in (2, 1, 3)]
+
+    def swap(w):
+        acc, sib, rs, half, mine, peer, *_ = waves[w]
         if w == 0:
-            f_twin.wait_recv()
-            f_across = go(f_all.at[x, z], f_all.at[x, z], f_s.at[1], f_r.at[1], across)
-
-    f_across.wait_recv()
-    piece = f_all.at[:, z]
-    f_far = [
-        go(piece, piece, f_s.at[2 + i], f_r.at[2 + i], chip(d)) for i, d in enumerate((8, 4, 12))
-    ]
-
-    def swap(w):
-        acc, sib, rs, mine, peer, *_ = waves[w]
-        for copy in parts[w]:
-            copy.wait_recv()
-        mine[...] = tree(rs[i] for i in range(Z))
-        return go(mine, peer, one_s.at[1, w], one_r.at[1, w], across)
+            arrive(direct)
+            mine[...] = tree(rs[i] for i in range(Z))
+        else:
+            arrive(far[w])
+            mine[...] = (half[high] + rs[12]) + (rs[13] + rs[14])
+        return go(mine, peer, swap_s.at[w], swap_r.at[w], across)
 
     sub = lax.broadcasted_iota(jnp.int32, (8, 128), 0)
     lane = lax.broadcasted_iota(jnp.int32, (8, 128), 1)
 
     def spread(w, swapped):
-        acc, sib, rs, mine, peer, s_all, rs_s, rs_r, ag_s, ag_r = waves[w]
+        acc, sib, rs, half, mine, peer, s_all, s_sem, r_sem = waves[w]
         swapped.wait_recv()
-        s_all[z] = mine[...] + peer[...]
+        s_all[strip] = mine[...] + peer[...]
         for q in range(K):
             if WAVE_OF[q, q][0] == w:
                 d = diag[:, 128 * q : 128 * q + 128]
                 d = jnp.broadcast_to(jnp.where(core == 0, d[0:1], d[1:2]), (8, 128))
-                s_all[z, WAVE_OF[q, q][1]] += jnp.where(lane == 8 * z + sub, d, 0.0)
+                s_all[strip, WAVE_OF[q, q][1]] += jnp.where(lane == 8 * strip + sub, d, 0.0)
+        own = s_all.at[strip]
+        if w == 0:
+            return [
+                go(own, own, s_sem.at[16 + d], r_sem.at[16 + d], chip(d)) for d in FAR_FIRST
+            ]
         return [
-            go(s_all.at[z], s_all.at[z], ag_s.at[d - 1], ag_r.at[d - 1], chip(d))
-            for d in FAR_FIRST
-        ]
-
-    swap0 = swap(0)
+            go(own, own, s_sem.at[5 + k], r_sem.at[5 + k], chip(4 * k)) for k in (2, 1, 3)
+        ]
+
+    def pass_on(w, copies):
+        s_all, s_sem, r_sem = waves[w][6:]
+        arrive(copies)
+        piece = s_all.at[pl.ds(4 * kind, 4)]
+        return [
+            go(piece, piece, s_sem.at[9 + i], r_sem.at[9 + i], chip(d))
+            for i, d in enumerate(near_by)
+        ]
+
+    gather0 = spread(0, swap(0))
     swap1 = swap(1)
-    gather0 = spread(0, swap0)
     swap2 = swap(2)
     gather1 = spread(1, swap1)
-    for copy in f_far:
-        copy.wait_recv()
-    f_near = []
-    for i, d in enumerate((15, 1, 2)):
-        for k in range(4):
-            piece = f_all.at[:, (z + 4 * k) % Z]
-            f_near.append(go(piece, piece, f2_s.at[i, k], f2_r.at[i, k], chip(d)))
     swap3 = swap(3)
     gather2 = spread(2, swap2)
     gather3 = spread(3, swap3)
-    gathers = (gather0, gather1, gather2, gather3)
-
-    def arrive(copies):
-        for copy in copies:
-            copy.wait_recv()
 
     def block(i, j):
         w, p = WAVE_OF[i, j]
-        return waves[w][5][:, p].reshape(128, 128)
+        return waves[w][6][:, p].reshape(128, 128)
 
     low[...] = jnp.zeros_like(low)
     us, invs = {}, []
@@ -300,6 +326,15 @@
         low[lo : lo + 128, lo : lo + 128] = u.T
         invs.append(split(inv))
         if q == 0:
+            gather1 = pass_on(1, gather1)
+            gather2 = pass_on(2, gather2)
+            gather3 = pass_on(3, gather3)
+            arrive(f_far)
+            piece = f_all.at[:, :, kind]
+            f_near = [
+                go(piece, piece, f_s.at[5 + i], f_r.at[5 + i], chip(d))
+                for i, d in enumerate(near_by)
+            ]
             arrive(gather1)
         for j in range(q + 1, K):
             v = mm(invs[q], split(block(0, j) if q == 0 else a[q, j]), NN)
@@ -311,17 +346,16 @@
                 a[1, j] = block(1, j) - mm(us[0, 1], us[0, j], TN)
         elif q == 1:
             arrive(gather3)
-            arrive(f_near)
             for i in range(2, K):
                 for j in range(i, K):
                     a[i, j] = block(i, j) - (
                         mm(us[0, i], us[0, j], TN) + mm(us[1, i], us[1, j], TN)
                     )
-            solve(0)
-            solve(1)
         elif q == 2:
             a[3, 3] -= mm(us[2, 3], us[2, 3], TN)
-            solve(2)
+            arrive(f_near)
+            for p in range(3):
+                solve(p)
         else:
             solve(3)
 
@@ -360,7 +394,7 @@
     ft = jnp.swapaxes(first_link, 1, 2)
     vmem = pl.BlockSpec(memory_space=pltpu.VMEM)
     smem = pl.BlockSpec(memory_space=pltpu.SMEM)
-    hbm = pl.BlockSpec(memory_space=pl.ANY)
+    hbm = pl.BlockSpec(memory_space=pltpu.HBM)
     dma = pltpu.SemaphoreType.DMA
     waves = []
     for wave in WAVES:
@@ -369,10 +403,13 @@
             pltpu.VMEM((2, Z, *tile), f32),
             pltpu.VMEM((Z, *tile), f32),
             pltpu.VMEM((Z, *tile), f32),
+            pltpu.VMEM((4, *tile), f32),
             pltpu.VMEM(tile, f32),
             pltpu.VMEM(tile, f32),
             pltpu.VMEM((Z, *tile), f32),
-        ] + [dma((Z - 1,))] * 4
+            dma((2 * Z,)),
+            dma((2 * Z,)),
+        ]
     return pl.pallas_call(
         functools.partial(kernel, groups),
         out_shape=[
@@ -384,19 +421,19 @@
         scratch_shapes=[
             pltpu.VMEM(link_blocks.shape, f32),
             pltpu.VMEM(inverse_blocks.shape, f32),
-            pltpu.VMEM((2, Z, 16, width), f32),
+            pltpu.VMEM((2, 4, 4, 16, width), f32),
             pltpu.VMEM((K, K, 128, 128), f32),
             pltpu.VMEM((width, width), f32),
             pltpu.VMEM((width, width), f32),
             pltpu.VMEM((4, 8, width), f32),
             pltpu.VMEM((2, groups, 8, width), f32),
             dma((2, link_blocks.shape[0])),
-            dma((2, len(WAVES))),
-            dma((2, len(WAVES))),
-            dma((5,)),
-            dma((5,)),
-            dma((3, 4)),
-            dma((3, 4)),
+            dma((len(WAVES),)),
+            dma((len(WAVES),)),
+            dma((len(WAVES),)),
+            dma((len(WAVES),)),
+            dma((8,)),
+            dma((8,)),
             dma((2 * groups,)),
             dma((2 * groups,)),
             *waves,

time: 130 us -> 98.9 us (0.76)
  Pallas kernels: 121 us -> 89.8 us
    pallas_call x1, Pallas kernels: 121 us -> 89.8 us  [shards(): pl.pallas_call(functools.partial(kernel, groups), out_shape=[jax.ShapeDty...]
where the time goes in v3:
time: 98.9 us; the launch traced here: 98.5 us
  Pallas kernels  89.8 us (91%)
  local copies, waits for them, and re-layouts  7.44 us (8%)
  between operations  1.3 us (1%)
    pallas_call x1, Pallas kernels, shards(): pl.pallas_call(functools.partial(kernel, groups), out_shape=[jax.ShapeDty...  89.8 us
    unnamed x16, local copies, waits for them, and re-layouts  7.44 us

profile of v3, /device:TPU:1, one launch (start us, length us, event | category | flops | bytes accessed | tf_op | source)
XLA Modules:
  0.0 98.5 jit_solution(1922732901501027636)
XLA Ops:
  1.3 0.0 copy-start
  1.3 1.6 %copy-done = f32[4,256,512]{2,1,0:T(8,128)S(1)} copy-done((f32[4,256,512]{2,1,0:T(8,128)S(1)}, f32[4,256,512]{2,1,0:T(8,128)}, u32[]{:S(2)}) %copy-start) | copy-done | bytes 2097176
  2.9 0.0 copy-start.1
  2.9 1.2 %copy-done.1 = f32[4,256,256]{2,1,0:T(8,128)S(1)} copy-done((f32[4,256,256]{2,1,0:T(8,128)S(1)}, f32[4,256,256]{2,1,0:T(8,128)}, u32[]{:S(2)}) %copy-start.1) | copy-done | bytes 1048600
  4.1 0.0 copy-start.2
  4.1 0.8 copy-done.2
  4.9 0.0 copy-start.3
  4.9 0.7 copy-done.3
  5.5 0.0 copy-start.4
  5.5 0.7 copy-done.4
  6.2 0.0 copy-start.5
  6.2 0.7 copy-done.5
  6.9 0.0 copy-start.6
  6.9 0.7 copy-done.6
  7.5 89.8 %schur.1 = (f32[2,8,512]{2,1,0:T(8,128)S(1)}, f32[8,512]{1,0:T(8,128)S(1)}) custom-call(s32[4]{0:T(128)S(1)} %copy-done.4, s32[4]{0:T(128)S(1)} %copy-done.5, s32[1]{0:T(128)S(6)} %copy.12.count, f32[8]{0:T(128)S(1)} %copy-done.6, f32[4,256,512]{2,1,0:T(8,128)S(1)} %copy-done, f32[4,256,256]{2,1,0:T(8,128)S(1)} %copy-done.1, f32[2,512]{1,0:T(2,128)S(1)} %copy-done.3, ...), custom_call_target="tpu_custom_call" | custom-call | tf_op jit(solution)/shard_map/schur/pallas_call | solution.py:413
  97.3 0.6 copy.13
  97.9 0.6 copy.14
Async XLA Ops:
  1.3 1.6 %copy-start = (f32[4,256,512]{2,1,0:T(8,128)S(1)}, f32[4,256,512]{2,1,0:T(8,128)}, u32[]{:S(2)}) copy-start(f32[4,256,512]{2,1,0:T(8,128)} %link_hbm.1) | copy-start | bytes 6291460
  2.9 1.2 %copy-start.1 = (f32[4,256,256]{2,1,0:T(8,128)S(1)}, f32[4,256,256]{2,1,0:T(8,128)}, u32[]{:S(2)}) copy-start(f32[4,256,256]{2,1,0:T(8,128)} %inverse_hbm.1) | copy-start | bytes 3145732
  4.1 0.8 copy-start.2
  4.9 0.7 copy-start.3
  5.5 0.7 copy-start.4
  6.2 0.7 copy-start.5
  6.9 0.7 copy-start.6

commit v4 on v3

--- a/solution.py
+++ b/solution.py
@@ -15,11 +15,11 @@
 K = 4
 WAVES = (
     ((0, 0),),
-    ((0, 1), (0, 2), (0, 3)),
-    ((1, 1), (1, 2), (1, 3)),
-    ((2, 2), (2, 3), (3, 3)),
+    ((0, 1), (0, 2), (0, 3), (1, 1)),
+    ((1, 2), (1, 3), (2, 2), (2, 3), (3, 3)),
 )
 WAVE_OF = {block: (w, i) for w, wave in enumerate(WAVES) for i, block in enumerate(wave)}
+DIRECT = 1
 FAR_FIRST = (8, 7, 9, 6, 10, 5, 11, 4, 12, 3, 13, 2, 14, 1, 15)
 MESH = pl.DeviceIdType.MESH
 
@@ -123,8 +123,8 @@
 
 
 def kernel(
-    groups, rows, nodes, count, fd, link_hbm, inverse_hbm, diag, ft, l_out, first_out,
-    link, inverse, f_all, a, xt, low, g_own, got, load, twin_s, twin_r, swap_s, swap_r,
+    groups, rows, nodes, count, fd, link, inverse, diag, ft, l_out, first_out,
+    f_all, f_peer, a, xt, low, l_own, g_own, got, twin_s, twin_r, swap_s, swap_r,
     f_s, f_r, end_s, end_r, *wave_refs,
 ):
     scen = lax.axis_index("scen")
@@ -140,24 +140,19 @@
     twin = {"scen": scen + 1 - 2 * core}
     across = {"scen": ((1 - x) * Z + z) * 2 + core}
     finals = []
-    for c in range(2):
-        for n in range(groups):
-            if c + n > 0:
-                to_core = (core + c) % 2
-                to = {"scen": scen - core + to_core, "node": (group + n) % groups}
-                finals.append((to_core, to))
+    for dx in range(2):
+        for c in range(2):
+            for n in range(groups):
+                if dx + c + n > 0:
+                    to_core, to_x = (core + c) % 2, (x + dx) % 2
+                    to = {"scen": (to_x * Z + z) * 2 + to_core, "node": (group + n) % groups}
+                    finals.append((dx, to_core, to))
     barrier = pltpu.get_barrier_semaphore()
-    greet = [chip(d) for d in range(1, Z)] + [across] + [to for _, to in finals]
+    greet = [chip(d) for d in range(1, Z)] + [to for *_, to in finals]
     for to in greet:
         pl.semaphore_signal(barrier, inc=1, device_id=to, device_id_type=MESH)
 
     slots = link.shape[0]
-    loads = []
-    for i in range(slots):
-        for n, (src, dst) in enumerate(((link_hbm, link), (inverse_hbm, inverse))):
-            loads.append(pltpu.make_async_copy(src.at[i], dst.at[i], load.at[n, i]))
-            loads[-1].start()
-
     per = len(wave_refs) // len(WAVES)
     waves = [wave_refs[per * w : per * w + per] for w in range(len(WAVES))]
     sent = []
@@ -175,8 +170,6 @@
     for acc, *_ in waves:
         acc[...] = jnp.zeros_like(acc)
     row_id = lax.broadcasted_iota(jnp.int32, (link.shape[1], 1), 0)
-    for copy in loads:
-        copy.wait()
 
     def slot(i, carry):
         limit = jnp.where(i < count[0], rows[i], 0)
@@ -206,25 +199,25 @@
     for w, (acc, sib, *_) in enumerate(waves):
         twins.append(go(acc.at[1 - core], sib, twin_s.at[w], twin_r.at[w], twin))
         if w == 0:
-            f_own = f_all.at[x, high, kind, pl.ds(core * 8, 8), :]
+            f_own = f_all.at[high, kind, pl.ds(core * 8, 8), :]
             f_twin = go(ft.at[1 - core], f_own, f_s.at[0], f_r.at[0], twin)
-    f_all[x, high, kind, pl.ds(core * 8, 8), :] = ft[core]
-
-    acc, sib, rs, _, mine0, peer0, s0, s_sem, r_sem = waves[0]
-    twins[0].wait_recv()
-    acc[core] += sib[...]
-    direct = []
-    for d in FAR_FIRST:
-        to = (z + d) % Z
-        direct.append(
-            go(acc.at[core, 4 * (to % 4) + to // 4], rs.at[z], s_sem.at[d], r_sem.at[d], chip(d))
-        )
-    rs[z] = acc[core, strip]
+    f_all[high, kind, pl.ds(core * 8, 8), :] = ft[core]
+
+    if DIRECT:
+        acc, sib, rs, _, mine0, peer0, s0, s_sem, r_sem = waves[0]
+        twins[0].wait_recv()
+        acc[core] += sib[...]
+        direct = []
+        for d in FAR_FIRST:
+            to = (z + d) % Z
+            direct.append(
+                go(acc.at[core, 4 * (to % 4) + to // 4], rs.at[z], s_sem.at[d], r_sem.at[d], chip(d))
+            )
+        rs[z] = acc[core, strip]
     f_twin.wait_recv()
-    f_own = f_all.at[x, high, kind]
-    f_across = go(f_own, f_own, f_s.at[1], f_r.at[1], across)
+    f_across = go(f_all.at[high, kind], f_peer, f_s.at[1], f_r.at[1], across)
     near = {}
-    for w in range(1, len(WAVES)):
+    for w in range(DIRECT, len(WAVES)):
         acc, sib, rs, half, mine, peer, s_all, s_sem, r_sem = waves[w]
         twins[w].wait_recv()
         acc[core] += sib[...]
@@ -236,7 +229,7 @@
             for i, d in enumerate(near_by)
         ]
     far = {}
-    for w in range(1, len(WAVES)):
+    for w in range(DIRECT, len(WAVES)):
         acc, sib, rs, half, mine, peer, s_all, s_sem, r_sem = waves[w]
         arrive(near[w])
         half[...] = (acc[core, pl.ds(4 * kind, 4)] + rs[0:4]) + (rs[4:8] + rs[8:12])
@@ -245,13 +238,12 @@
             for k in (2, 1, 3)
         ]
 
-    f_across.wait_recv()
-    piece = f_all.at[:, high, kind]
+    piece = f_all.at[high, kind]
     f_far = [go(piece, piece, f_s.at[1 + k], f_r.at[1 + k], chip(4 * k)) for k in (2, 1, 3)]
 
     def swap(w):
         acc, sib, rs, half, mine, peer, *_ = waves[w]
-        if w == 0:
+        if w < DIRECT:
             arrive(direct)
             mine[...] = tree(rs[i] for i in range(Z))
         else:
@@ -272,7 +264,7 @@
                 d = jnp.broadcast_to(jnp.where(core == 0, d[0:1], d[1:2]), (8, 128))
                 s_all[strip, WAVE_OF[q, q][1]] += jnp.where(lane == 8 * strip + sub, d, 0.0)
         own = s_all.at[strip]
-        if w == 0:
+        if w < DIRECT:
             return [
                 go(own, own, s_sem.at[16 + d], r_sem.at[16 + d], chip(d)) for d in FAR_FIRST
             ]
@@ -289,13 +281,15 @@
             for i, d in enumerate(near_by)
         ]
 
-    gather0 = spread(0, swap(0))
-    swap1 = swap(1)
-    swap2 = swap(2)
-    gather1 = spread(1, swap1)
-    swap3 = swap(3)
-    gather2 = spread(2, swap2)
-    gather3 = spread(3, swap3)
+    gathers = {}
+    if DIRECT:
+        gathers[0] = spread(0, swap(0))
+    swaps = {}
+    for w in range(DIRECT, len(WAVES)):
+        swaps[w] = swap(w)
+        if w - 1 in swaps:
+            gathers[w - 1] = spread(w - 1, swaps[w - 1])
+    gathers[w] = spread(w, swaps[w])
 
     def block(i, j):
         w, p = WAVE_OF[i, j]
@@ -303,49 +297,61 @@
 
     low[...] = jnp.zeros_like(low)
     us, invs = {}, []
+    own_half = xt.shape[0] - 16
+
+    def columns(lo):
+        half = f_all[...].reshape(own_half, -1)[:, lo : lo + 128]
+        return jnp.concatenate([half, f_peer[:, lo : lo + 128]], 0)
 
     def solve(q):
         lo = 128 * q
-        src = xt
-        if q == 0:
-            part = f_all[...].reshape(4 * 128, -1)[:, lo : lo + 128]
-        else:
-            part = xt[:, lo : lo + 128]
-        xq = mm(split(part), invs[q], NT)
+        xq = mm(split(columns(lo) if q == 0 else xt[:, lo : lo + 128]), invs[q], NT)
         xs = split(xq)
         for j in range(q + 1, K):
             hi = 128 * j
-            old = f_all[...].reshape(4 * 128, -1)[:, hi : hi + 128] if q == 0 else xt[:, hi : hi + 128]
+            old = columns(hi) if q == 0 else xt[:, hi : hi + 128]
             xt[:, hi : hi + 128] = old - mm(xs, us[q, j], NN)
         xt[:, lo : lo + 128] = xq
 
-    arrive(gather0)
+    done = set()
+
+    def ready(row):
+        for j in range(row, K):
+            w = WAVE_OF[row, j][0]
+            if w not in done:
+                done.add(w)
+                arrive(gathers[w])
+
+    if not DIRECT:
+        gathers[0] = pass_on(0, gathers[0])
+    arrive(gathers[0])
+    done.add(0)
     for q in range(K):
         lo = 128 * q
         u, inv = diag_block(block(0, 0) if q == 0 else a[q, q])
         low[lo : lo + 128, lo : lo + 128] = u.T
         invs.append(split(inv))
         if q == 0:
-            gather1 = pass_on(1, gather1)
-            gather2 = pass_on(2, gather2)
-            gather3 = pass_on(3, gather3)
+            for w in range(1, len(WAVES)):
+                gathers[w] = pass_on(w, gathers[w])
             arrive(f_far)
-            piece = f_all.at[:, :, kind]
+            piece = f_all.at[:, kind]
             f_near = [
                 go(piece, piece, f_s.at[5 + i], f_r.at[5 + i], chip(d))
                 for i, d in enumerate(near_by)
             ]
-            arrive(gather1)
+            ready(0)
         for j in range(q + 1, K):
             v = mm(invs[q], split(block(0, j) if q == 0 else a[q, j]), NN)
             low[128 * j : 128 * j + 128, lo : lo + 128] = v.T
             us[q, j] = split(v)
         if q == 0:
-            arrive(gather2)
+            ready(1)
             for j in range(1, K):
                 a[1, j] = block(1, j) - mm(us[0, 1], us[0, j], TN)
         elif q == 1:
-            arrive(gather3)
+            ready(2)
+            ready(3)
             for i in range(2, K):
                 for j in range(i, K):
                     a[i, j] = block(i, j) - (
@@ -353,7 +359,7 @@
                     )
         elif q == 2:
             a[3, 3] -= mm(us[2, 3], us[2, 3], TN)
-            arrive(f_near)
+            arrive(f_near + [f_across])
             for p in range(3):
                 solve(p)
         else:
@@ -361,25 +367,30 @@
 
     own = pl.multiple_of((x * Z + z) * 16, 16)
     width = first_out.shape[1]
-    g_own[0] = low[pl.ds(own, 8), :]
-    g_own[1] = low[pl.ds(pl.multiple_of(own + 8, 8), 8), :]
-    factor = go(g_own.at[1 - core], l_out.at[core], end_s.at[0], end_r.at[0], twin)
-    l_out[core] = g_own[core]
-    term = mm(split(xt[pl.ds(own, 16), :]), split(xt[...]), NT)
-    g_own[2] = term[:8]
-    g_own[3] = term[8:]
+    l_own[0] = low[pl.ds(own, 8), :]
+    l_own[1] = low[pl.ds(pl.multiple_of(own + 8, 8), 8), :]
+    factor = go(l_own.at[1 - core], l_out.at[core], end_s.at[0], end_r.at[0], twin)
+    l_out[core] = l_own[core]
+    wanted = jnp.concatenate([xt[pl.ds(pl.multiple_of(16 * z, 16), 16), :], xt[own_half:, :]], 0)
+    term = mm(split(wanted), split(xt[:own_half, :]), NT)
+    for dx in range(2):
+        for c in range(2):
+            lo = 16 * dx + 8 * c
+            g_own[dx, c] = term[lo : lo + 8]
     last = [
-        go(g_own.at[2 + to_core], got.at[core, group], end_s.at[1 + i], end_r.at[1 + i], to)
-        for i, (to_core, to) in enumerate(finals)
+        go(g_own.at[dx, to_core], got.at[x, core, group], end_s.at[1 + i], end_r.at[1 + i], to)
+        for i, (dx, to_core, to) in enumerate(finals)
     ]
-    got[core, group] = g_own[2 + core]
+    got[x, core, group] = g_own[0, core]
     arrive(last)
     row8 = lax.broadcasted_iota(jnp.int32, (8, width), 0)
     col8 = lax.broadcasted_iota(jnp.int32, (8, width), 1)
     d = jnp.zeros((8, width), f32)
     for i in range(8):
         d = jnp.where(row8 == i, fd[i], d)
-    total = tree(got[c, n] for c in range(2) for n in range(groups))
+    total = jnp.concatenate(
+        [tree(got[h, c, n] for c in range(2) for n in range(groups)) for h in range(2)], 1
+    )
     first_out[...] = total + jnp.where(col8 == scen * 8 + row8, d, 0.0)
     factor.wait_recv()
     for copy in sent:
@@ -394,7 +405,6 @@
     ft = jnp.swapaxes(first_link, 1, 2)
     vmem = pl.BlockSpec(memory_space=pltpu.VMEM)
     smem = pl.BlockSpec(memory_space=pltpu.SMEM)
-    hbm = pl.BlockSpec(memory_space=pltpu.HBM)
     dma = pltpu.SemaphoreType.DMA
     waves = []
     for wave in WAVES:
@@ -416,26 +426,25 @@
             jax.ShapeDtypeStruct((2, 8, width), f32),
             jax.ShapeDtypeStruct((8, width), f32),
         ],
-        in_specs=[smem] * 4 + [hbm] * 2 + [vmem] * 2,
+        in_specs=[smem] * 4 + [vmem] * 4,
         out_specs=[vmem] * 2,
         scratch_shapes=[
-            pltpu.VMEM(link_blocks.shape, f32),
-            pltpu.VMEM(inverse_blocks.shape, f32),
-            pltpu.VMEM((2, 4, 4, 16, width), f32),
+            pltpu.VMEM((4, 4, 16, width), f32),
+            pltpu.VMEM((16, width), f32),
             pltpu.VMEM((K, K, 128, 128), f32),
+            pltpu.VMEM((width // 2 + 16, width), f32),
             pltpu.VMEM((width, width), f32),
-            pltpu.VMEM((width, width), f32),
-            pltpu.VMEM((4, 8, width), f32),
-            pltpu.VMEM((2, groups, 8, width), f32),
-            dma((2, link_blocks.shape[0])),
+            pltpu.VMEM((2, 8, width), f32),
+            pltpu.VMEM((2, 2, 8, width // 2), f32),
+            pltpu.VMEM((2, 2, groups, 8, width // 2), f32),
             dma((len(WAVES),)),
             dma((len(WAVES),)),
             dma((len(WAVES),)),
             dma((len(WAVES),)),
             dma((8,)),
             dma((8,)),
-            dma((2 * groups,)),
-            dma((2 * groups,)),
+            dma((4 * groups,)),
+            dma((4 * groups,)),
             *waves,
         ],
         compiler_params=pltpu.CompilerParams(

time: 98.9 us -> 93.1 us (0.941)
  Pallas kernels: 89.8 us -> 84 us
    pallas_call x1, Pallas kernels: 89.8 us -> 84 us  [shards(): pl.pallas_call(functools.partial(kernel, groups), out_shape=[jax.ShapeDty...]
where the time goes in v4:
time: 93.1 us; the launch traced here: 92.8 us
  Pallas kernels  84 us (90%)
  local copies, waits for them, and re-layouts  7.44 us (8%)
  between operations  1.3 us (1%)
    pallas_call x1, Pallas kernels, shards(): pl.pallas_call(functools.partial(kernel, groups), out_shape=[jax.ShapeDty...  84 us
    unnamed x16, local copies, waits for them, and re-layouts  7.44 us

profile of v4, /device:TPU:1, one launch (start us, length us, event | category | flops | bytes accessed | tf_op | source)
XLA Modules:
  0.0 92.8 jit_solution(11099936707429537152)
XLA Ops:
  1.3 0.0 copy-start
  1.3 1.6 %copy-done = f32[4,256,512]{2,1,0:T(8,128)S(1)} copy-done((f32[4,256,512]{2,1,0:T(8,128)S(1)}, f32[4,256,512]{2,1,0:T(8,128)}, u32[]{:S(2)}) %copy-start) | copy-done | bytes 2097176
  2.9 0.0 copy-start.1
  2.9 1.2 %copy-done.1 = f32[4,256,256]{2,1,0:T(8,128)S(1)} copy-done((f32[4,256,256]{2,1,0:T(8,128)S(1)}, f32[4,256,256]{2,1,0:T(8,128)}, u32[]{:S(2)}) %copy-start.1) | copy-done | bytes 1048600
  4.1 0.0 copy-start.2
  4.1 0.8 copy-done.2
  4.9 0.0 copy-start.3
  4.9 0.7 copy-done.3
  5.5 0.0 copy-start.4
  5.5 0.7 copy-done.4
  6.2 0.0 copy-start.5
  6.2 0.7 copy-done.5
  6.9 0.0 copy-start.6
  6.9 0.7 copy-done.6
  7.5 84.0 %schur.1 = (f32[2,8,512]{2,1,0:T(8,128)S(1)}, f32[8,512]{1,0:T(8,128)S(1)}) custom-call(s32[4]{0:T(128)S(1)} %copy-done.4, s32[4]{0:T(128)S(1)} %copy-done.5, s32[1]{0:T(128)S(6)} %copy.12.count, f32[8]{0:T(128)S(1)} %copy-done.6, f32[4,256,512]{2,1,0:T(8,128)S(1)} %copy-done, f32[4,256,256]{2,1,0:T(8,128)S(1)} %copy-done.1, f32[2,512]{1,0:T(2,128)S(1)} %copy-done.3, ...), custom_call_target="tpu_custom_call" | custom-call | tf_op jit(solution)/shard_map/schur/pallas_call | solution.py:423
  91.5 0.6 copy.13
  92.2 0.6 copy.14
Async XLA Ops:
  1.3 1.6 %copy-start = (f32[4,256,512]{2,1,0:T(8,128)S(1)}, f32[4,256,512]{2,1,0:T(8,128)}, u32[]{:S(2)}) copy-start(f32[4,256,512]{2,1,0:T(8,128)} %link.1) | copy-start | bytes 6291460
  2.9 1.2 %copy-start.1 = (f32[4,256,256]{2,1,0:T(8,128)S(1)}, f32[4,256,256]{2,1,0:T(8,128)}, u32[]{:S(2)}) copy-start(f32[4,256,256]{2,1,0:T(8,128)} %inverse.1) | copy-start | bytes 3145732
  4.1 0.8 copy-start.2
  4.9 0.7 copy-start.3
  5.5 0.7 copy-start.4
  6.2 0.7 copy-start.5
  6.9 0.7 copy-start.6

commit v5 on v4

--- a/solution.py
+++ b/solution.py
@@ -123,8 +123,8 @@
 
 
 def kernel(
-    groups, rows, nodes, count, fd, link, inverse, diag, ft, l_out, first_out,
-    f_all, f_peer, a, xt, low, l_own, g_own, got, twin_s, twin_r, swap_s, swap_r,
+    groups, rows, nodes, count, fd, link_hbm, inverse_hbm, diag, ft, l_out, first_out,
+    link, inverse, load, f_all, f_peer, a, xt, low, l_own, g_own, got, twin_s, twin_r, swap_s, swap_r,
     f_s, f_r, end_s, end_r, *wave_refs,
 ):
     scen = lax.axis_index("scen")
@@ -153,6 +153,12 @@
         pl.semaphore_signal(barrier, inc=1, device_id=to, device_id_type=MESH)
 
     slots = link.shape[0]
+    loads = []
+    for i in range(slots):
+        for n, (src, dst) in enumerate(((link_hbm, link), (inverse_hbm, inverse))):
+            loads.append(pltpu.make_async_copy(src.at[i], dst.at[i], load.at[n, i]))
+            loads[-1].start()
+
     per = len(wave_refs) // len(WAVES)
     waves = [wave_refs[per * w : per * w + per] for w in range(len(WAVES))]
     sent = []
@@ -170,6 +176,8 @@
     for acc, *_ in waves:
         acc[...] = jnp.zeros_like(acc)
     row_id = lax.broadcasted_iota(jnp.int32, (link.shape[1], 1), 0)
+    for copy in loads:
+        copy.wait()
 
     def slot(i, carry):
         limit = jnp.where(i < count[0], rows[i], 0)
@@ -405,6 +413,7 @@
     ft = jnp.swapaxes(first_link, 1, 2)
     vmem = pl.BlockSpec(memory_space=pltpu.VMEM)
     smem = pl.BlockSpec(memory_space=pltpu.SMEM)
+    hbm = pl.BlockSpec(memory_space=pltpu.HBM)
     dma = pltpu.SemaphoreType.DMA
     waves = []
     for wave in WAVES:
@@ -426,9 +435,12 @@
             jax.ShapeDtypeStruct((2, 8, width), f32),
             jax.ShapeDtypeStruct((8, width), f32),
         ],
-        in_specs=[smem] * 4 + [vmem] * 4,
+        in_specs=[smem] * 4 + [hbm] * 2 + [vmem] * 2,
         out_specs=[vmem] * 2,
         scratch_shapes=[
+            pltpu.VMEM(link_blocks.shape, f32),
+            pltpu.VMEM(inverse_blocks.shape, f32),
+            dma((2, link_blocks.shape[0])),
             pltpu.VMEM((4, 4, 16, width), f32),
             pltpu.VMEM((16, width), f32),
             pltpu.VMEM((K, K, 128, 128), f32),
@@ -453,7 +465,9 @@
         name="schur",
     )(
         block_rows, node_of, slot_count, first_diag,
-        link_blocks, inverse_blocks, node_diag, ft,
+        pltpu.with_memory_space_constraint(link_blocks, pltpu.HBM),
+        pltpu.with_memory_space_constraint(inverse_blocks, pltpu.HBM),
+        node_diag, ft,
     )
 
 

time: 93.1 us -> 88.5 us (0.951)
  local copies, waits for them, and re-layouts: 7.44 us -> 4.62 us
  Pallas kernels: 84 us -> 82.3 us
    unnamed x16 -> x12, local copies, waits for them, and re-layouts: 7.44 us -> 4.62 us
    pallas_call x1, Pallas kernels: 84 us -> 82.3 us  [shards(): pl.pallas_call(functools.partial(kernel, groups), out_shape=[jax.ShapeDty...]
where the time goes in v5:
time: 88.5 us; the launch traced here: 88.2 us
  Pallas kernels  82.3 us (93%)
  local copies, waits for them, and re-layouts  4.62 us (5%)
  between operations  1.3 us (1%)
    pallas_call x1, Pallas kernels, shards(): pl.pallas_call(functools.partial(kernel, groups), out_shape=[jax.ShapeDty...  82.3 us
    unnamed x12, local copies, waits for them, and re-layouts  4.62 us

profile of v5, /device:TPU:1, one launch (start us, length us, event | category | flops | bytes accessed | tf_op | source)
XLA Modules:
  0.0 88.2 jit_solution(11844810603559993568)
XLA Ops:
  1.3 0.0 copy-start
  1.3 0.7 copy-done
  2.0 0.0 copy-start.1
  2.0 0.7 copy-done.1
  2.7 0.0 copy-start.2
  2.7 0.7 copy-done.2
  3.4 0.0 copy-start.3
  3.4 0.7 copy-done.3
  4.0 0.0 copy-start.4
  4.0 0.7 copy-done.4
  4.7 82.3 %schur.1 = (f32[2,8,512]{2,1,0:T(8,128)S(1)}, f32[8,512]{1,0:T(8,128)S(1)}) custom-call(s32[4]{0:T(128)S(1)} %copy-done.2, s32[4]{0:T(128)S(1)} %copy-done.3, s32[1]{0:T(128)S(6)} %copy.12.count, f32[8]{0:T(128)S(1)} %copy-done.4, f32[4,256,512]{2,1,0:T(8,128)} %link_hbm.1, f32[4,256,256]{2,1,0:T(8,128)} %inverse_hbm.1, f32[2,512]{1,0:T(2,128)S(1)} %copy-done.1, ...), custom_call_target="tpu_custom_call" | custom-call | tf_op jit(solution)/shard_map/schur/pallas_call | solution.py:432
  87.0 0.6 copy.13
  87.6 0.6 copy.14
Async XLA Ops:
  1.3 0.8 copy-start
  2.0 0.7 copy-start.1
  2.7 0.7 copy-start.2
  3.4 0.7 copy-start.3
  4.0 0.7 copy-start.4

commit v6 on v5

--- a/solution.py
+++ b/solution.py
@@ -153,11 +153,9 @@
         pl.semaphore_signal(barrier, inc=1, device_id=to, device_id_type=MESH)
 
     slots = link.shape[0]
-    loads = []
     for i in range(slots):
         for n, (src, dst) in enumerate(((link_hbm, link), (inverse_hbm, inverse))):
-            loads.append(pltpu.make_async_copy(src.at[i], dst.at[i], load.at[n, i]))
-            loads[-1].start()
+            pltpu.make_async_copy(src.at[i], dst.at[i], load.at[n, i]).start()
 
     per = len(wave_refs) // len(WAVES)
     waves = [wave_refs[per * w : per * w + per] for w in range(len(WAVES))]
@@ -176,10 +174,10 @@
     for acc, *_ in waves:
         acc[...] = jnp.zeros_like(acc)
     row_id = lax.broadcasted_iota(jnp.int32, (link.shape[1], 1), 0)
-    for copy in loads:
-        copy.wait()
 
     def slot(i, carry):
+        pltpu.make_async_copy(link_hbm.at[i], link.at[i], load.at[0, i]).wait()
+        pltpu.make_async_copy(inverse_hbm.at[i], inverse.at[i], load.at[1, i]).wait()
         limit = jnp.where(i < count[0], rows[i], 0)
         masked = jnp.where(row_id < limit, link[i], 0.0)
         first = nodes[i] == 2 * group

time: 88.5 us -> 88.4 us (level)
  no operation moved by 1% of the time
where the time goes in v6:
time: 88.4 us; the launch traced here: 88.1 us
  Pallas kernels  82.2 us (93%)
  local copies, waits for them, and re-layouts  4.62 us (5%)
  between operations  1.3 us (1%)
    pallas_call x1, Pallas kernels, shards(): pl.pallas_call(functools.partial(kernel, groups), out_shape=[jax.ShapeDty...  82.2 us
    unnamed x12, local copies, waits for them, and re-layouts  4.62 us

profile of v6, /device:TPU:1, one launch (start us, length us, event | category | flops | bytes accessed | tf_op | source)
XLA Modules:
  0.0 88.1 jit_solution(14016610534325182438)
XLA Ops:
  1.3 0.0 copy-start
  1.3 0.7 copy-done
  2.0 0.0 copy-start.1
  2.0 0.7 copy-done.1
  2.7 0.0 copy-start.2
  2.7 0.7 copy-done.2
  3.4 0.0 copy-start.3
  3.4 0.7 copy-done.3
  4.0 0.0 copy-start.4
  4.0 0.7 copy-done.4
  4.7 82.2 %schur.1 = (f32[2,8,512]{2,1,0:T(8,128)S(1)}, f32[8,512]{1,0:T(8,128)S(1)}) custom-call(s32[4]{0:T(128)S(1)} %copy-done.2, s32[4]{0:T(128)S(1)} %copy-done.3, s32[1]{0:T(128)S(6)} %copy.12.count, f32[8]{0:T(128)S(1)} %copy-done.4, f32[4,256,512]{2,1,0:T(8,128)} %link_hbm.1, f32[4,256,256]{2,1,0:T(8,128)} %inverse_hbm.1, f32[2,512]{1,0:T(2,128)S(1)} %copy-done.1, ...), custom_call_target="tpu_custom_call" | custom-call | tf_op jit(solution)/shard_map/schur/pallas_call | solution.py:430
  86.9 0.6 copy.13
  87.5 0.6 copy.14
Async XLA Ops:
  1.3 0.8 copy-start
  2.0 0.7 copy-start.1
  2.7 0.7 copy-start.2
  3.4 0.7 copy-start.3
  4.0 0.7 copy-start.4
